TPU v7x, 512 devices: a whole 4x8x8 slice. The times are simulated.
512 devices in a mesh: grp: 16 (over y, core), ops: 32 (over x, z).
Axes of the slice: x: 4, y: 8, z: 8, core: 2. Of those that a mesh axis runs over, the one named last changes fastest.
Arguments:
- op_embed: bfloat16 [131072, 256], P(('grp', 'ops')), may hold values from -6 to 6
- machine_embed: bfloat16 [8192, 256], P('grp'), may hold values from -6 to 6
- cotangent: bfloat16 [131072, 256], P(('grp', 'ops')), may hold values from -6 to 6
- w_query: bfloat16 [256, 256], replicated, may hold values from -0.375 to 0.375
- w_key: bfloat16 [256, 256], replicated, may hold values from -0.375 to 0.375
- w_value: bfloat16 [256, 256], replicated, may hold values from -0.375 to 0.375
- slot_local: int32 [512, 16], P(('grp', 'ops')), may hold values from 0 to 3
- counts: int32 [131072, 16], P(('grp', 'ops')), may hold values from 0 to 128, as said below
Outputs:
- op_grad: bfloat16 [131072, 256], P(('grp', 'ops'))
- machine_grad: float32 [8192, 256], P(('grp', 'ops'))
- grad_wq: float32 [256, 256], replicated
- grad_wk: float32 [256, 256], replicated
- grad_wv: float32 [256, 256], replicated
Inputs may be any that keep to these rules, and one draw needn't show every extreme that they name: The eligible machines of slot e's block for operation o are its first counts[o, e] machines; 0 means the operation has no eligible machine in that block.
All inputs are finite; a program needn't handle non-finite values.
Results may differ from a plain program's by a relative error of at most 0.0056.
Values may be sent and summed in bfloat16 or wider, within the bound.
No kernel may reach another device: no remote copies, remote signals or barrier semaphores. Data moves between devices by JAX's collectives and lax.ppermute only.
A program may use at most 64 MiB of HBM per device.

v0:
```python
import jax
import jax.numpy as jnp
from jax import lax
from jax.sharding import PartitionSpec as P

HEADS = 8
BLK = 128


mean_scale = 0.08838834764831845


def slot_grads(queries, cotangent4, key_rows, value_rows, lengths):
    head_size = queries.shape[2]
    inv_root = head_size ** (-0.5)
    scores = (
        jnp.einsum("ohc,mhc->ohm", queries, key_rows, preferred_element_type=jnp.float32) * inv_root
    )
    sigmoid_score = jax.nn.sigmoid(scores)
    columns = lax.broadcasted_iota(jnp.int32, scores.shape, 2)
    eligible = columns < lengths[:, None, None]
    gates = jnp.where(eligible, sigmoid_score, 0.0).astype(jnp.bfloat16)
    value_dot = jnp.einsum(
        "ohc,mhc->ohm", cotangent4, value_rows, preferred_element_type=jnp.float32
    )
    dscore = jnp.where(
        eligible, mean_scale * value_dot * sigmoid_score * (1.0 - sigmoid_score) * inv_root, 0.0
    ).astype(jnp.bfloat16)
    query_part = jnp.einsum("ohm,mhc->ohc", dscore, key_rows, preferred_element_type=jnp.float32)
    key_grad = jnp.einsum(
        "ohm,ohc->mhc", dscore, queries, preferred_element_type=jnp.float32
    ).astype(jnp.bfloat16)
    value_grad = (
        mean_scale
        * jnp.einsum("ohm,ohc->mhc", gates, cotangent4, preferred_element_type=jnp.float32)
    ).astype(jnp.bfloat16)
    return (query_part, key_grad, value_grad)


def per_device(op_embed, machine_embed, cotangent, w_query, w_key, w_value, slot_local, counts):
    groups = lax.axis_size("grp")
    ops_count = op_embed.shape[0]
    model_width = op_embed.shape[1]
    head_size = model_width // HEADS
    machine_rows = machine_embed.shape[0]
    blocks_here = machine_rows // BLK
    highest = lax.Precision.HIGHEST
    both_weights = jnp.concatenate([w_key, w_value], axis=1)
    queries = jnp.dot(op_embed, w_query, preferred_element_type=jnp.float32).astype(jnp.bfloat16)
    wanted = lax.all_to_all(
        slot_local.reshape(groups, 1), "grp", split_axis=0, concat_axis=0, tiled=True
    )
    wanted_ids = wanted[:, 0]
    picker = wanted_ids[:, None] == jnp.arange(blocks_here, dtype=jnp.int32)[None, :]
    local_pairs = jnp.dot(machine_embed, both_weights, preferred_element_type=jnp.float32).astype(
        jnp.bfloat16
    )
    outgoing = local_pairs.reshape(blocks_here, BLK, 2 * model_width)[wanted_ids]
    fetched = lax.all_to_all(outgoing, "grp", split_axis=0, concat_axis=0, tiled=True)
    key_slots = fetched[:, :, :model_width].reshape(groups, BLK, HEADS, head_size)
    value_slots = fetched[:, :, model_width:].reshape(groups, BLK, HEADS, head_size)
    query_heads = queries.reshape(ops_count, HEADS, head_size)
    cot_heads = cotangent.reshape(ops_count, HEADS, head_size)

    def per_slot(summed_q, pieces):
        key_rows, value_rows, lengths = pieces
        query_part, key_grad, value_grad = slot_grads(
            query_heads, cot_heads, key_rows, value_rows, lengths
        )
        return (
            summed_q + query_part,
            (key_grad.reshape(BLK, model_width), value_grad.reshape(BLK, model_width)),
        )

    start_q = jnp.zeros((ops_count, HEADS, head_size), jnp.float32)
    summed_q, (key_grads, value_grads) = lax.scan(
        per_slot, start_q, (key_slots, value_slots, counts.T)
    )
    grad_query = summed_q.astype(jnp.bfloat16).reshape(ops_count, model_width)
    op_grad = (
        cotangent.astype(jnp.float32)
        + jnp.dot(grad_query, w_query.T, preferred_element_type=jnp.float32)
    ).astype(jnp.bfloat16)
    wq_term = jnp.einsum("od,oe->de", op_embed, grad_query, preferred_element_type=jnp.float32)
    returned = lax.all_to_all(
        jnp.concatenate([key_grads, value_grads], axis=2),
        "grp",
        split_axis=0,
        concat_axis=0,
        tiled=True,
    )
    summed = jnp.einsum(
        "gb,gr->br",
        picker.astype(jnp.bfloat16),
        returned.reshape(groups, BLK * 2 * model_width),
        preferred_element_type=jnp.float32,
    )
    summed = summed.reshape(machine_rows, 2 * model_width)
    key_total = summed[:, :model_width]
    value_total = summed[:, model_width:]
    machine_part = jnp.dot(key_total, w_key.astype(jnp.float32).T, precision=highest) + jnp.dot(
        value_total, w_value.astype(jnp.float32).T, precision=highest
    )
    embed_f = machine_embed.astype(jnp.float32)
    wk_term = jnp.dot(embed_f.T, key_total, precision=highest)
    wv_term = jnp.dot(embed_f.T, value_total, precision=highest)
    summed_total = lax.psum(machine_part, "ops")
    share_rows = machine_rows // lax.axis_size("ops")
    first_row = lax.axis_index("ops") * share_rows
    machine_grad = lax.dynamic_slice_in_dim(summed_total, first_row, share_rows, 0)
    weight_sums = lax.psum((wq_term, wk_term, wv_term), ("grp", "ops"))
    shard_count = float(groups * lax.axis_size("ops"))
    grad_wq = weight_sums[0] / shard_count
    grad_wk = weight_sums[1] / shard_count
    grad_wv = weight_sums[2] / shard_count
    return (op_grad, machine_grad, grad_wq, grad_wk, grad_wv)


def solution(mesh):
    return jax.shard_map(
        per_device,
        mesh=mesh,
        in_specs=(
            P(("grp", "ops"), None),
            P("grp", None),
            P(("grp", "ops"), None),
            P(),
            P(),
            P(),
            P(("grp", "ops"), None),
            P(("grp", "ops"), None),
        ),
        out_specs=(P(("grp", "ops"), None), P(("grp", "ops"), None), P(), P(), P()),
        check_vma=False,
    )
```

profile of v0, /device:TPU:1, one launch (start us, length us, event | category | flops | bytes accessed | tf_op | source)
XLA Modules:
  0.0 653.7 jit_solution(9235457132968034616)
XLA Ops:
  7.2 1.4 copy.46
  8.6 10.1 %all-to-all-start = ((s32[16,1,1]{2,1,0:T(1,128)}), s32[16,1,1]{2,1,0:T(1,128)S(1)}, u32[]{:S(2)}, u32[]{:S(2)}) async-start(s32[16,1,1]{2,1,0:T(1,128)} %copy.46), calls=%async_computation | async-start | bytes 16384 | tf_op jit(solution)/shard_map/all_to_all | solution.py:50
  19.9 5.7 all-to-all-done
  26.1 2.0 gather_fusion
  28.1 4.3 all-to-all-start.1
  32.8 48.7 %all-to-all-done.1 = bf16[16,128,512]{2,1,0:T(8,128)(2,1)S(1)} async-done(((bf16[16,128,512]{2,1,0:T(8,128)(2,1)}), bf16[16,128,512]{2,1,0:T(8,128)(2,1)S(1)}, u32[]{:S(2)}, u32[]{:S(2)}) %all-to-all-start.1) | async-done | bytes 2097184 | tf_op jit(solution)/shard_map/all_to_all | solution.py:59
  81.5 1.6 fusion.38
  83.1 1.7 copy.47
  84.8 1.3 copy.48
  86.1 63.6 %while.15 = (s32[]{:T(128)}, f32[256,8,32]{0,2,1:T(8,128)S(1)}, bf16[16,128,256]{1,2,0:T(8,128)(2,1)}, bf16[16,128,256]{1,2,0:T(8,128)(2,1)}, bf16[16,128,8,32]{...) while((s32[]{:T(128)}, f32[256,8,32]{0,2,1:T(8,128)S(1)}, ...), condition=%wide.region_1.2_spmd.clone, body=%wide.region_0.1_spmd.clone.sunk | while | flops 87785472 | bytes 6361235 | solution.py:76
  87.4 1.3 fusion.80
  91.3 1.3 fusion.80
  103.3 1.3 fusion.80
  131.1 1.3 fusion.80
  135.1 1.3 fusion.80
  143.0 1.3 fusion.80
  147.0 1.3 fusion.80
  149.7 3.1 pad_maximum_fusion
  152.8 5.0 all-to-all-start.2
  158.8 48.2 %all-to-all-done.2 = bf16[16,128,512]{1,2,0:T(8,128)(2,1)} async-done(((bf16[16,128,512]{1,2,0:T(8,128)(2,1)}), bf16[16,128,512]{1,2,0:T(8,128)(2,1)}, u32[]{:S(2)}, u32[]{:S(2)}) %all-to-all-start.2) | async-done | bytes 2097184 | tf_op jit(solution)/shard_map/all_to_all | solution.py:85
  207.0 3.4 copy.57
  216.9 272.9 %all-reduce.6.cloned.1.call-done = (f32[256,256]{0,1:T(8,128)}, f32[256,256]{0,1:T(8,128)}, f32[256,256]{0,1:T(8,128)}) async-done(((f32[256,256]{0,1:T(8,128)}, f32[256,256]{0,1:T(8,128)}, f32[256,256]{0,1:T(8,128)}), (f32[256,256]{0,1:T(8,128)}, f32[256,256]{0,1:T(8,128)}, f32[256,256]{0,1:T(8,128)})) %all-reduce.6.cloned.1.call-update) | async-done | bytes 786448 | tf_op jit(solution)/shard_map/psum | solution.py:111
  494.4 151.2 %all-reduce.4.cloned.1.call-done = f32[512,256]{1,0:T(8,128)} async-done(((f32[512,256]{1,0:T(8,128)}), f32[512,256]{1,0:T(8,128)}) %all-reduce.4.cloned.1.call-update) | async-done | bytes 524304 | tf_op jit(solution)/shard_map/psum | solution.py:107
  645.6 1.3 constant_dynamic-slice_fusion.1
  (152 shorter events, 68.0 us)
Async XLA Ops:
  7.2 11.5 %copy-start = (bf16[512,256]{1,0:T(8,128)(2,1)S(1)}, bf16[512,256]{1,0:T(8,128)(2,1)}, u32[]{:S(2)}) copy-start(bf16[512,256]{1,0:T(8,128)(2,1)} %param.11) | copy-start | bytes 786436
  8.6 17.1 %all-to-all-start = ((s32[16,1,1]{2,1,0:T(1,128)}), s32[16,1,1]{2,1,0:T(1,128)S(1)}, u32[]{:S(2)}, u32[]{:S(2)}) async-start(s32[16,1,1]{2,1,0:T(1,128)} %copy.46), calls=%async_computation | async-start | bytes 16384 | tf_op jit(solution)/shard_map/all_to_all | solution.py:50
  28.1 4.3 copy-start.6
  28.1 4.5 copy-start.2
  28.1 4.5 copy-start.4
  28.1 53.4 %all-to-all-start.1 = ((bf16[16,128,512]{2,1,0:T(8,128)(2,1)}), bf16[16,128,512]{2,1,0:T(8,128)(2,1)S(1)}, u32[]{:S(2)}, u32[]{:S(2)}) async-start(bf16[16,128,512]{2,1,0:T(8,128)(2,1)} %gather_fusion), calls=%async_computation.1 | async-start | bytes 4194304 | tf_op jit(solution)/shard_map/all_to_all | solution.py:59
  83.1 1.7 copy-start.1
  152.8 5.0 copy-start.3
  152.8 54.1 %all-to-all-start.2 = ((bf16[16,128,512]{1,2,0:T(8,128)(2,1)}), bf16[16,128,512]{1,2,0:T(8,128)(2,1)}, u32[]{:S(2)}, u32[]{:S(2)}) async-start(bf16[16,128,512]{1,2,0:T(8,128)(2,1)} %pad_maximum_fusion), calls=%async_computation.2 | async-start | bytes 4194304 | tf_op jit(solution)/shard_map/all_to_all | solution.py:85
  157.8 332.0 %all-reduce.6.cloned.1.call-start = ((), (), s32[]{:S(2)}) async-start(), calls=%async_computation.4 | async-start | bytes 1572864 | tf_op jit(solution)/shard_map/psum | solution.py:111
  210.9 3.4 copy-start.8
  211.6 3.1 copy-start.9
  214.2 1.8 copy-start.5
  214.2 1.8 copy-start.7
  214.3 431.3 %all-reduce.4.cloned.1.call-start = ((), (), s32[]{:S(2)}) async-start(), calls=%async_computation.3 | async-start | bytes 1048576 | tf_op jit(solution)/shard_map/psum | solution.py:107
Sparse Core Ops, SparseCore 0:
  214.4 275.4 all-reduce.5
  493.2 152.2 all-reduce.3
where the time goes:
time: 659 us; the launch traced here: 654 us
  waiting for transfers between devices  527 us (80%)
  matrix products  48.8 us (7%)
  local copies, waits for them, and re-layouts  38.4 us (6%)
  starting transfers between devices  19.5 us (3%)
  between operations  14.3 us (2%)
    psum x1, waiting for transfers between devices, per_device(): weight_sums = lax.psum((wq_term, wk_term, wv_term), ('grp', 'ops'))  273 us
    psum x1, waiting for transfers between devices, per_device(): summed_total = lax.psum(machine_part, 'ops')  151 us
    all_to_all x1, waiting for transfers between devices, per_device(): lax.all_to_all(outgoing, 'grp', split_axis=0, concat_axis=0, tiled=True)  48.7 us
    all_to_all x1, waiting for transfers between devices, per_device(): lax.all_to_all(jnp.concatenate([key_grads, value_grads], axis=2), 'grp',...  48.2 us
    dot_general x16, matrix products, slot_grads(): jnp.einsum('ohc,mhc->ohm', cotangent4, value_rows, preferred_element_type...  20.9 us
  transfers between devices with their start and end apart: 5, of which 5 were waited for; matrix products, arithmetic and copies ran while one was open for 1% of the time, Pallas kernels for 0%

commit v1 on v0

v1 whole, which is shorter than its diff:
```python
import functools

import jax
import jax.numpy as jnp
from jax import lax
from jax.experimental import pallas as pl
from jax.experimental.pallas import tpu as pltpu
from jax.sharding import PartitionSpec as P

HEADS = 8
BLK = 128
MEAN_SCALE = 0.08838834764831845

f32 = jnp.float32
bf16 = jnp.bfloat16
VMEM_SPEC = pl.BlockSpec(memory_space=pltpu.VMEM)
SMEM_SPEC = pl.BlockSpec(memory_space=pltpu.SMEM)


def dot(a, b):
    return jnp.dot(a, b, preferred_element_type=f32)


def dot_nt(a, b):
    return lax.dot_general(a, b, (((1,), (1,)), ((), ())), preferred_element_type=f32)


def dot_tn(a, b):
    return lax.dot_general(a, b, (((0,), (0,)), ((), ())), preferred_element_type=f32)


def attend_kernel(
    rows_ref,
    counts_ref,
    op_ref,
    cot_ref,
    wq_ref,
    wk_ref,
    wv_ref,
    wkt_ref,
    back_ref,
    opg_ref,
    wgrad_ref,
    qm_ref,
    cm_ref,
    gq_ref,
):
    step = pl.program_id(0)
    slots, blk, width = rows_ref.shape
    ops_count = op_ref.shape[0]
    head_size = width // HEADS
    inv_root = head_size ** (-0.5)
    machines = slots * blk

    @pl.when(step == 0)
    def _():
        queries = dot(op_ref[...], wq_ref[...]).astype(bf16)
        cot = cot_ref[...]
        lane_head = lax.broadcasted_iota(jnp.int32, (ops_count, width), 1) // head_size
        zero = jnp.zeros((), bf16)
        for h in range(HEADS):
            here = lane_head == h
            qm_ref[pl.ds(h * ops_count, ops_count), :] = jnp.where(here, queries, zero)
            cm_ref[pl.ds(h * ops_count, ops_count), :] = jnp.where(here, cot, zero)
        gq_ref[...] = jnp.zeros_like(gq_ref)
        wgrad_ref[pl.ds(width, 2 * width), :] = jnp.zeros((2 * width, width), f32)

    embed = rows_ref[...].reshape(machines, width)
    keys = dot(embed, wk_ref[...]).astype(bf16)
    values = dot(embed, wv_ref[...]).astype(bf16)
    keys_t = dot_nt(wkt_ref[...], embed).astype(bf16)
    place = lax.broadcasted_iota(jnp.int32, (blk, ops_count), 0)
    eligible = jnp.concatenate(
        [place < counts_ref[s, 0:1, :] for s in range(slots)], axis=0
    )
    key_grad = jnp.zeros((machines, width), f32)
    value_grad = jnp.zeros((machines, width), f32)
    for h in range(HEADS):
        q_h = qm_ref[pl.ds(h * ops_count, ops_count), :]
        c_h = cm_ref[pl.ds(h * ops_count, ops_count), :]
        scores = dot_nt(keys, q_h)
        value_dot = dot_nt(values, c_h)
        half = jnp.tanh(scores * (0.5 * inv_root))
        gate2 = jnp.where(eligible, 1.0 + half, 0.0).astype(bf16)
        slope = jnp.where(eligible, value_dot * (1.0 - half * half), 0.0).astype(bf16)
        key_grad += dot(slope, q_h)
        value_grad += dot(gate2, c_h)
        gq_ref[pl.ds(h * head_size, head_size), :] += dot(
            keys_t[h * head_size : (h + 1) * head_size, :], slope
        )
    d_scale = 0.25 * MEAN_SCALE * inv_root
    key_grad = (key_grad * d_scale).astype(bf16)
    value_grad = (value_grad * (0.5 * MEAN_SCALE)).astype(bf16)
    back = dot_nt(key_grad, wk_ref[...]) + dot_nt(value_grad, wv_ref[...])
    back_ref[...] = back.reshape(slots, blk, width).astype(bf16)
    wgrad_ref[pl.ds(width, width), :] += dot_tn(embed, key_grad)
    wgrad_ref[pl.ds(2 * width, width), :] += dot_tn(embed, value_grad)

    @pl.when(step == pl.num_programs(0) - 1)
    def _():
        grad_query = (gq_ref[...] * d_scale).T.astype(bf16)
        opg_ref[...] = (
            cot_ref[...].astype(f32) + dot_nt(grad_query, wq_ref[...])
        ).astype(bf16)
        wgrad_ref[pl.ds(0, width), :] = dot_tn(op_ref[...], grad_query)


def attend(rows, counts_t, op_embed, cotangent, w_query, w_key, w_value):
    slots, blk, width = rows.shape
    ops_count = op_embed.shape[0]
    pair = 2
    full = lambda shape: pl.BlockSpec(shape, lambda i: (0,) * len(shape))
    steps = slots // pair
    weight = full((width, width))
    return pl.pallas_call(
        attend_kernel,
        grid=(steps,),
        in_specs=[
            pl.BlockSpec((pair, blk, width), lambda i: (i, 0, 0)),
            pl.BlockSpec((pair, 1, ops_count), lambda i: (i, 0, 0)),
            full((ops_count, width)),
            full((ops_count, width)),
            weight,
            weight,
            weight,
            weight,
        ],
        out_specs=[
            pl.BlockSpec((pair, blk, width), lambda i: (i, 0, 0)),
            full((ops_count, width)),
            full((3 * width, width)),
        ],
        out_shape=[
            jax.ShapeDtypeStruct((slots, blk, width), bf16),
            jax.ShapeDtypeStruct((ops_count, width), bf16),
            jax.ShapeDtypeStruct((3 * width, width), f32),
        ],
        scratch_shapes=[
            pltpu.VMEM((HEADS * ops_count, width), bf16),
            pltpu.VMEM((HEADS * ops_count, width), bf16),
            pltpu.VMEM((width, ops_count), f32),
        ],
        compiler_params=pltpu.CompilerParams(dimension_semantics=("arbitrary",)),
        name="attend",
    )(
        rows,
        counts_t.reshape(slots, 1, ops_count),
        op_embed,
        cotangent,
        w_query,
        w_key,
        w_value,
        w_key.T,
    )


def pick_kernel(ids_ref, blocks_ref, out_ref):
    for g in range(out_ref.shape[0]):
        out_ref[g] = blocks_ref[ids_ref[g]]


def pick_blocks(ids, blocks):
    return pl.pallas_call(
        pick_kernel,
        in_specs=[SMEM_SPEC, VMEM_SPEC],
        out_specs=VMEM_SPEC,
        out_shape=jax.ShapeDtypeStruct((ids.shape[0],) + blocks.shape[1:], blocks.dtype),
        name="pick_blocks",
    )(ids, blocks)


def collect_kernel(ids_ref, parts_ref, out_ref, acc_ref):
    acc_ref[...] = jnp.zeros_like(acc_ref)
    for g in range(parts_ref.shape[0]):
        acc_ref[ids_ref[g]] += parts_ref[g].astype(f32)
    out_ref[...] = acc_ref[...].astype(out_ref.dtype)


def collect_blocks(ids, parts, blocks):
    shape = (blocks,) + parts.shape[1:]
    return pl.pallas_call(
        collect_kernel,
        in_specs=[SMEM_SPEC, VMEM_SPEC],
        out_specs=VMEM_SPEC,
        out_shape=jax.ShapeDtypeStruct(shape, bf16),
        scratch_shapes=[pltpu.VMEM(shape, f32)],
        name="collect_blocks",
    )(ids, parts)


def swap(x, axis):
    return lax.all_to_all(x, axis, split_axis=0, concat_axis=0, tiled=True)


def per_device(op_embed, machine_embed, cotangent, w_query, w_key, w_value, slot_local, counts):
    groups = lax.axis_size("grp")
    shards = lax.axis_size("ops")
    width = op_embed.shape[1]
    machine_rows = machine_embed.shape[0]
    blocks_here = machine_rows // BLK
    ids = swap(slot_local.reshape(groups, 1), "grp")[:, 0]
    outgoing = pick_blocks(ids, machine_embed.reshape(blocks_here, BLK, width))
    rows = swap(outgoing, "grp")
    back, op_grad, wgrad = attend(
        rows, counts.T, op_embed, cotangent, w_query, w_key, w_value
    )
    returned = swap(back, "grp")
    group_sum = collect_blocks(ids, returned, blocks_here)
    shares = swap(group_sum.reshape(shards, machine_rows // shards, width), "ops")
    machine_grad = jnp.sum(shares.astype(f32), axis=0)

    lead = 3 * width // shards
    scattered = swap(wgrad.astype(bf16).reshape(shards, lead, width), "ops")
    part = jnp.sum(scattered.astype(f32), axis=0).astype(bf16)
    crossed = swap(jnp.broadcast_to(part[None], (groups, lead, width)), "grp")
    mean = jnp.sum(crossed.astype(f32), axis=0) * (1.0 / (groups * shards))
    spread = swap(
        jnp.broadcast_to(mean.astype(bf16)[None], (shards, lead, width)), "ops"
    )
    total = spread.astype(f32).reshape(3, width, width)
    return (op_grad, machine_grad, total[0], total[1], total[2])


def solution(mesh):
    return jax.shard_map(
        per_device,
        mesh=mesh,
        in_specs=(
            P(("grp", "ops"), None),
            P("grp", None),
            P(("grp", "ops"), None),
            P(),
            P(),
            P(),
            P(("grp", "ops"), None),
            P(("grp", "ops"), None),
        ),
        out_specs=(P(("grp", "ops"), None), P(("grp", "ops"), None), P(), P(), P()),
        check_vma=False,
    )
```

time: 659 us -> 189 us (0.29)
  waiting for transfers between devices: 527 us -> 74.7 us
  blocking collectives: 0 us -> 56.2 us
  matrix products: 48.8 us -> 0 us
  local copies, waits for them, and re-layouts: 38.4 us -> 4.82 us
  Pallas kernels: 0 us -> 28.9 us
  between operations: 14.3 us -> 0.71 us
    psum x2 -> x0, waiting for transfers between devices: 424 us -> none  [the longest x1 273 us: per_device(): weight_sums = lax.psum((wq_term, wk_term, wv_term), ('grp', 'ops'))]
    all_to_all x0 -> x3, blocking collectives: none -> 56.2 us  [swap(): return lax.all_to_all(x, axis, split_axis=0, concat_axis=0, tiled=True)]
    dot_general x89 -> x0, matrix products: 48.8 us -> none  [the longest x16 20.9 us: slot_grads(): jnp.einsum('ohc,mhc->ohm', cotangent4, value_rows, preferred_element_type...]
    pallas_call x0 -> x3, Pallas kernels: none -> 28.9 us  [the longest x1 24.7 us: attend(): pl.pallas_call(attend_kernel, grid=(steps,), in_specs=[pl.BlockSpec((pair...]
    all_to_all x3 -> x4, waiting for transfers between devices: 103 us -> 74.7 us  [swap(): return lax.all_to_all(x, axis, split_axis=0, concat_axis=0, tiled=True)]
    dynamic_slice x17 -> x0, local copies, waits for them, and re-layouts: 12.6 us -> none  [the longest x16 11.3 us: per_device(): lax.scan(per_slot, start_q, (key_slots, value_slots, counts.T))]
    dynamic_update_slice x16 -> x0, local copies, waits for them, and re-layouts: 11 us -> none  [per_device(): lax.scan(per_slot, start_q, (key_slots, value_slots, counts.T))]
    all_to_all x3 -> x4, starting transfers between devices: 19.4 us -> 18.3 us  [swap(): return lax.all_to_all(x, axis, split_axis=0, concat_axis=0, tiled=True)]
  transfers between devices with their start and end apart: 5 -> 4, of which waited for: 5 -> 4; matrix products, arithmetic and copies ran while one was open for 1% -> 1% of each run, Pallas kernels for 0% -> 1%
where the time goes in v1:
time: 189 us; the launch traced here: 186 us
  waiting for transfers between devices  74.7 us (40%)
  blocking collectives  56.2 us (30%)
  Pallas kernels  28.9 us (15%)
  starting transfers between devices  18.3 us (10%)
  local copies, waits for them, and re-layouts  4.82 us (3%)
  other arithmetic  2.89 us (2%)
    all_to_all x4, waiting for transfers between devices, swap(): return lax.all_to_all(x, axis, split_axis=0, concat_axis=0, tiled=True)  74.7 us
    all_to_all x3, blocking collectives, swap(): return lax.all_to_all(x, axis, split_axis=0, concat_axis=0, tiled=True)  56.2 us
    pallas_call x1, Pallas kernels, attend(): pl.pallas_call(attend_kernel, grid=(steps,), in_specs=[pl.BlockSpec((pair...  24.7 us
    all_to_all x4, starting transfers between devices, swap(): return lax.all_to_all(x, axis, split_axis=0, concat_axis=0, tiled=True)  18.3 us
  transfers between devices with their start and end apart: 4, of which 4 were waited for; matrix products, arithmetic and copies ran while one was open for 1% of the time, Pallas kernels for 1%

profile of v1, /device:TPU:1, one launch (start us, length us, event | category | flops | bytes accessed | tf_op | source)
XLA Modules:
  0.0 186.4 jit_solution(9457751546383142660)
XLA Ops:
  0.6 0.6 copy-done.4
  1.3 0.1 copy.18
  1.4 16.3 %all_to_all.39 = s32[16,1,1]{2,1,0:T(1,128)S(1)} all-to-all(s32[16,1,1]{2,1,0:T(1,128)S(1)} %copy.18), channel_id=1, replica_groups=mesh['grp'=16,'ops'=32] {'grp'}, dimensions={0} | all-to-all | bytes 128 | tf_op jit(solution)/shard_map/all_to_all | solution.py:192
  17.7 0.9 reduce.1.ids_ref
  18.6 2.0 %pick_blocks.1 = bf16[16,128,256]{2,1,0:T(8,128)(2,1)} custom-call(s32[16]{0:T(128)} %reduce.1.ids_ref, bf16[4,128,256]{2,1,0:T(8,128)(2,1)} %bitcast.18), custom_call_target="tpu_custom_call" | custom-call | tf_op jit(solution)/shard_map/pick_blocks/pallas_call | solution.py:163
  20.6 4.2 %all-to-all-start.1 = ((bf16[16,128,256]{2,1,0:T(8,128)(2,1)}), bf16[16,128,256]{2,1,0:T(8,128)(2,1)S(1)}, u32[]{:S(2)}, u32[]{:S(2)}) async-start(bf16[16,128,256]{2,1,0:T(8,128)(2,1)} %pick_blocks.1), calls=%async_computation.1 | async-start | bytes 2097152 | tf_op jit(solution)/shard_map/all_to_all | solution.py:192
  24.8 0.6 reshape.39.counts_ref
  25.4 0.8 copy.19
  26.2 26.7 %all-to-all-done.1.rows_ref = bf16[16,128,256]{2,1,0:T(8,128)(2,1)S(1)} async-done(((bf16[16,128,256]{2,1,0:T(8,128)(2,1)}), bf16[16,128,256]{2,1,0:T(8,128)(2,1)S(1)}, u32[]{:S(2)}, u32[]{:S(2)}) %all-to-all-start.1) | async-done | bytes 1048608 | tf_op jit(solution)/shard_map/all_to_all | solution.py:192
  52.9 1.0 copy-done
  53.8 24.7 %attend.1 = (bf16[16,128,256]{2,1,0:T(8,128)(2,1)}, bf16[256,256]{1,0:T(8,128)(2,1)}, f32[768,256]{1,0:T(8,128)}) custom-call(bf16[16,128,256]{2,1,0:T(8,128)(2,1)} %copy-done, s32[16,1,256]{2,1,0:T(1,128)} %reshape.39.counts_ref, bf16[256,256]{1,0:T(8,128)(2,1)} %op_ref.1, bf16[256,256]{1,0:T(8,128)(2,1)} %cot_ref.1, bf16[256,256]{1,0:T(8,128)(2,1)} %wq_ref.1, ...), custom_call_target="tpu_custom_call" | custom-call | tf_op jit(solution)/shard_map/attend/pallas_call | solution.py:115
  78.5 1.2 convert_element_type.20
  79.7 25.7 %all_to_all.40 = bf16[32,24,256]{2,1,0:T(8,128)(2,1)S(1)} all-to-all(bf16[32,24,256]{2,1,0:T(8,128)(2,1)S(1)} %bitcast.15), channel_id=1, replica_groups=mesh['grp'=16,'ops'=32] {'ops'}, dimensions={0} | all-to-all | bytes 786432 | tf_op jit(solution)/shard_map/all_to_all | solution.py:192
  105.5 14.2 %all_to_all.41 = bf16[16,24,256]{2,1,0:T(8,128)(2,1)S(1)} all-to-all(bf16[16,24,256]{2,1,0:T(8,128)(2,1)S(1)} %broadcast_in_dim.4), channel_id=1, replica_groups=mesh['grp'=16,'ops'=32] {'grp'}, dimensions={0} | all-to-all | bytes 393216 | tf_op jit(solution)/shard_map/all_to_all | solution.py:192
  119.7 3.6 %all-to-all-start.2 = ((bf16[16,128,256]{2,1,0:T(8,128)(2,1)}), bf16[16,128,256]{2,1,0:T(8,128)(2,1)S(1)}, u32[]{:S(2)}, u32[]{:S(2)}) async-start(bf16[16,128,256]{2,1,0:T(8,128)(2,1)} %get-tuple-element.9), calls=%async_computation.2 | async-start | bytes 2097152 | tf_op jit(solution)/shard_map/all_to_all | solution.py:192
  123.3 27.6 %all-to-all-done.2.parts_ref = bf16[16,128,256]{2,1,0:T(8,128)(2,1)S(1)} async-done(((bf16[16,128,256]{2,1,0:T(8,128)(2,1)}), bf16[16,128,256]{2,1,0:T(8,128)(2,1)S(1)}, u32[]{:S(2)}, u32[]{:S(2)}) %all-to-all-start.2) | async-done | bytes 1048608 | tf_op jit(solution)/shard_map/all_to_all | solution.py:192
  150.9 0.8 broadcast_in_dim.5
  151.7 5.3 %all-to-all-start.6 = ((bf16[32,24,256]{2,1,0:T(8,128)(2,1)}), bf16[32,24,256]{2,1,0:T(8,128)(2,1)S(1)}, u32[]{:S(2)}, u32[]{:S(2)}) async-start(bf16[32,24,256]{2,1,0:T(8,128)(2,1)} %broadcast_in_dim.5), calls=%async_computation.6 | async-start | bytes 786432 | tf_op jit(solution)/shard_map/all_to_all | solution.py:192
  157.0 2.2 %collect_blocks.1 = bf16[4,128,256]{2,1,0:T(8,128)(2,1)} custom-call(s32[16]{0:T(128)} %reduce.1.ids_ref, bf16[16,128,256]{2,1,0:T(8,128)(2,1)} %copy-done.1), custom_call_target="tpu_custom_call" | custom-call | tf_op jit(solution)/shard_map/collect_blocks/pallas_call | solution.py:181
  159.2 11.7 %all-to-all-done.6 = bf16[32,24,256]{2,1,0:T(8,128)(2,1)S(1)} async-done(((bf16[32,24,256]{2,1,0:T(8,128)(2,1)}), bf16[32,24,256]{2,1,0:T(8,128)(2,1)S(1)}, u32[]{:S(2)}, u32[]{:S(2)}) %all-to-all-start.6) | async-done | bytes 393248 | tf_op jit(solution)/shard_map/all_to_all | solution.py:192
  170.9 5.2 %all-to-all-start.3 = ((bf16[32,16,256]{2,1,0:T(8,128)(2,1)}), bf16[32,16,256]{2,1,0:T(8,128)(2,1)S(1)}, u32[]{:S(2)}, u32[]{:S(2)}) async-start(bf16[32,16,256]{2,1,0:T(8,128)(2,1)} %bitcast.16), calls=%async_computation.3 | async-start | bytes 524288 | tf_op jit(solution)/shard_map/all_to_all | solution.py:192
  176.2 0.9 slice_bitcast_fusion
  177.1 8.7 %all-to-all-done.3 = bf16[32,16,256]{2,1,0:T(8,128)(2,1)S(1)} async-done(((bf16[32,16,256]{2,1,0:T(8,128)(2,1)}), bf16[32,16,256]{2,1,0:T(8,128)(2,1)S(1)}, u32[]{:S(2)}, u32[]{:S(2)}) %all-to-all-start.3) | async-done | bytes 262176 | tf_op jit(solution)/shard_map/all_to_all | solution.py:192
  185.8 0.7 convert_reduce_fusion
  (13 shorter events, 0.2 us)
Async XLA Ops:
  0.6 0.7 copy-start.4
  20.6 4.2 %copy-start.3 = (s32[256,16]{0,1:T(8,128)S(1)}, s32[256,16]{0,1:T(8,128)}, u32[]{:S(2)}) copy-start(s32[256,16]{0,1:T(8,128)} %param.15) | copy-start | bytes 49156
  20.6 4.9 %copy-start.2 = (bf16[256,256]{1,0:T(8,128)(2,1)S(1)}, bf16[256,256]{1,0:T(8,128)(2,1)}, u32[]{:S(2)}) copy-start(bf16[256,256]{1,0:T(8,128)(2,1)} %wk_ref.1) | copy-start | bytes 393220
  20.6 32.3 %all-to-all-start.1 = ((bf16[16,128,256]{2,1,0:T(8,128)(2,1)}), bf16[16,128,256]{2,1,0:T(8,128)(2,1)S(1)}, u32[]{:S(2)}, u32[]{:S(2)}) async-start(bf16[16,128,256]{2,1,0:T(8,128)(2,1)} %pick_blocks.1), calls=%async_computation.1 | async-start | bytes 2097152 | tf_op jit(solution)/shard_map/all_to_all | solution.py:192
  52.9 1.0 copy-start
  119.7 31.2 %all-to-all-start.2 = ((bf16[16,128,256]{2,1,0:T(8,128)(2,1)}), bf16[16,128,256]{2,1,0:T(8,128)(2,1)S(1)}, u32[]{:S(2)}, u32[]{:S(2)}) async-start(bf16[16,128,256]{2,1,0:T(8,128)(2,1)} %get-tuple-element.9), calls=%async_computation.2 | async-start | bytes 2097152 | tf_op jit(solution)/shard_map/all_to_all | solution.py:192
  150.9 6.1 %copy-start.1 = (bf16[16,128,256]{2,1,0:T(8,128)(2,1)}, bf16[16,128,256]{2,1,0:T(8,128)(2,1)S(1)}, u32[]{:S(2)}) copy-start(bf16[16,128,256]{2,1,0:T(8,128)(2,1)S(1)} %all-to-all-done.2.parts_ref) | copy-start | bytes 3145732
  151.7 19.2 %all-to-all-start.6 = ((bf16[32,24,256]{2,1,0:T(8,128)(2,1)}), bf16[32,24,256]{2,1,0:T(8,128)(2,1)S(1)}, u32[]{:S(2)}, u32[]{:S(2)}) async-start(bf16[32,24,256]{2,1,0:T(8,128)(2,1)} %broadcast_in_dim.5), calls=%async_computation.6 | async-start | bytes 786432 | tf_op jit(solution)/shard_map/all_to_all | solution.py:192
  170.9 14.9 %all-to-all-start.3 = ((bf16[32,16,256]{2,1,0:T(8,128)(2,1)}), bf16[32,16,256]{2,1,0:T(8,128)(2,1)S(1)}, u32[]{:S(2)}, u32[]{:S(2)}) async-start(bf16[32,16,256]{2,1,0:T(8,128)(2,1)} %bitcast.16), calls=%async_computation.3 | async-start | bytes 524288 | tf_op jit(solution)/shard_map/all_to_all | solution.py:192

commit v2 on v1

v2 whole, which is shorter than its diff:
```python
import functools

import jax
import jax.numpy as jnp
from jax import lax
from jax.experimental import pallas as pl
from jax.experimental.pallas import tpu as pltpu
from jax.sharding import PartitionSpec as P

HEADS = 8
BLK = 128
MEAN_SCALE = 0.08838834764831845

f32 = jnp.float32
bf16 = jnp.bfloat16
VMEM_SPEC = pl.BlockSpec(memory_space=pltpu.VMEM)
SMEM_SPEC = pl.BlockSpec(memory_space=pltpu.SMEM)


def dot(a, b):
    return jnp.dot(a, b, preferred_element_type=f32)


def dot_nt(a, b):
    return lax.dot_general(a, b, (((1,), (1,)), ((), ())), preferred_element_type=f32)


def dot_tn(a, b):
    return lax.dot_general(a, b, (((0,), (0,)), ((), ())), preferred_element_type=f32)


def attend_kernel(
    rows_ref,
    counts_ref,
    op_ref,
    cot_ref,
    wq_ref,
    wk_ref,
    wv_ref,
    wkt_ref,
    back_ref,
    opg_ref,
    wgrad_ref,
    qm_ref,
    cm_ref,
    gq_ref,
    wkv_ref,
):
    slots, blk, width = rows_ref.shape
    ops_count = op_ref.shape[0]
    head_size = width // HEADS
    inv_root = head_size ** (-0.5)
    d_scale = 0.25 * MEAN_SCALE * inv_root
    pair = 2
    machines = pair * blk

    queries = dot(op_ref[...], wq_ref[...]).astype(bf16)
    cot = cot_ref[...]
    lane_head = lax.broadcasted_iota(jnp.int32, (ops_count, width), 1) // head_size
    zero = jnp.zeros((), bf16)
    for h in range(HEADS):
        here = lane_head == h
        qm_ref[pl.ds(h * ops_count, ops_count), :] = jnp.where(here, queries, zero)
        cm_ref[pl.ds(h * ops_count, ops_count), :] = jnp.where(here, cot, zero)
    gq_ref[...] = jnp.zeros_like(gq_ref)
    wkv_ref[...] = jnp.zeros_like(wkv_ref)

    def one_pair(step, carry):
        first = step * pair
        embed = rows_ref[pl.ds(first, pair)].reshape(machines, width)
        keys = dot(embed, wk_ref[...]).astype(bf16)
        values = dot(embed, wv_ref[...]).astype(bf16)
        keys_t = dot_nt(wkt_ref[...], embed).astype(bf16)
        place = lax.broadcasted_iota(jnp.int32, (blk, ops_count), 0)
        eligible = jnp.concatenate(
            [place < counts_ref[first + s] for s in range(pair)], axis=0
        )
        key_grad = jnp.zeros((machines, width), f32)
        value_grad = jnp.zeros((machines, width), f32)
        for h in range(HEADS):
            q_h = qm_ref[pl.ds(h * ops_count, ops_count), :]
            c_h = cm_ref[pl.ds(h * ops_count, ops_count), :]
            scores = dot_nt(keys, q_h)
            value_dot = dot_nt(values, c_h)
            half = jnp.tanh(scores * (0.5 * inv_root))
            gate2 = jnp.where(eligible, 1.0 + half, 0.0).astype(bf16)
            slope = jnp.where(eligible, value_dot * (1.0 - half * half), 0.0).astype(bf16)
            key_grad += dot(slope, q_h)
            value_grad += dot(gate2, c_h)
            gq_ref[pl.ds(h * head_size, head_size), :] += dot(
                keys_t[h * head_size : (h + 1) * head_size, :], slope
            )
        key_grad = (key_grad * d_scale).astype(bf16)
        value_grad = (value_grad * (0.5 * MEAN_SCALE)).astype(bf16)
        back = dot_nt(key_grad, wk_ref[...]) + dot_nt(value_grad, wv_ref[...])
        back = back.astype(bf16)
        for s in range(pair):
            back_ref[first + s, 0:blk, :] = back[s * blk : (s + 1) * blk]
        wkv_ref[0:width, :] += dot_tn(embed, key_grad)
        wkv_ref[width : 2 * width, :] += dot_tn(embed, value_grad)
        return carry

    lax.fori_loop(0, slots // pair, one_pair, 0)
    grad_query = (gq_ref[...] * d_scale).T.astype(bf16)
    opg_ref[...] = (cot.astype(f32) + dot_nt(grad_query, wq_ref[...])).astype(bf16)
    wgrad_ref[0:width, :] = dot_tn(op_ref[...], grad_query).astype(bf16)
    wgrad_ref[width : 3 * width, :] = wkv_ref[...].astype(bf16)


def attend(rows, counts_t, op_embed, cotangent, w_query, w_key, w_value, extra=0):
    slots, blk, width = rows.shape
    ops_count = op_embed.shape[0]
    return pl.pallas_call(
        attend_kernel,
        in_specs=[VMEM_SPEC] * 8,
        out_specs=[VMEM_SPEC] * 3,
        out_shape=[
            jax.ShapeDtypeStruct((slots, blk + extra, width), bf16),
            jax.ShapeDtypeStruct((ops_count, width), bf16),
            jax.ShapeDtypeStruct((3 * width, width), bf16),
        ],
        scratch_shapes=[
            pltpu.VMEM((HEADS * ops_count, width), bf16),
            pltpu.VMEM((HEADS * ops_count, width), bf16),
            pltpu.VMEM((width, ops_count), f32),
            pltpu.VMEM((2 * width, width), f32),
        ],
        name="attend",
    )(
        rows,
        counts_t.reshape(slots, 1, ops_count),
        op_embed,
        cotangent,
        w_query,
        w_key,
        w_value,
        w_key.T,
    )


def pick_kernel(ids_ref, blocks_ref, out_ref):
    for g in range(out_ref.shape[0]):
        out_ref[g] = blocks_ref[ids_ref[g]]


def pick_blocks(ids, blocks):
    return pl.pallas_call(
        pick_kernel,
        in_specs=[SMEM_SPEC, VMEM_SPEC],
        out_specs=VMEM_SPEC,
        out_shape=jax.ShapeDtypeStruct((ids.shape[0],) + blocks.shape[1:], blocks.dtype),
        name="pick_blocks",
    )(ids, blocks)


def fill_kernel(parts_ref, buffer_ref, out_ref, sum_ref, sems):
    sum_ref[...] = jnp.sum(parts_ref[...].astype(f32), axis=0).astype(bf16)
    groups, rows, width = out_ref.shape
    lead = sum_ref.shape[0]
    copies = [
        pltpu.make_async_copy(
            sum_ref, out_ref.at[g, pl.ds(rows - lead, lead), :], sems.at[g]
        )
        for g in range(groups)
    ]
    for copy in copies:
        copy.start()
    for copy in copies:
        copy.wait()


def fill_tail(parts, buffer):
    groups = buffer.shape[0]
    return pl.pallas_call(
        fill_kernel,
        in_specs=[VMEM_SPEC, pl.BlockSpec(memory_space=pl.ANY)],
        out_specs=pl.BlockSpec(memory_space=pl.ANY),
        out_shape=jax.ShapeDtypeStruct(buffer.shape, buffer.dtype),
        scratch_shapes=[
            pltpu.VMEM(parts.shape[1:], bf16),
            pltpu.SemaphoreType.DMA((groups,)),
        ],
        input_output_aliases={1: 0},
        name="fill_tail",
    )(parts, buffer)


def collect_kernel(ids_ref, parts_ref, out_ref, acc_ref):
    shards, rows, width = out_ref.shape
    blocks, blk, _ = acc_ref.shape
    share = blocks * blk // shards
    lead = rows - share
    groups = parts_ref.shape[0]
    acc_ref[...] = jnp.zeros_like(acc_ref)
    total = jnp.zeros((lead, width), f32)
    for g in range(groups):
        acc_ref[ids_ref[g]] += parts_ref[g, 0:blk, :].astype(f32)
        total += parts_ref[g, blk : blk + lead, :].astype(f32)
    total = (total * (1.0 / (groups * shards))).astype(bf16)
    for s in range(shards):
        at = s * share
        out_ref[s, 0:share, :] = acc_ref[at // blk, at % blk : at % blk + share, :].astype(
            bf16
        )
        out_ref[s, share:rows, :] = total


def collect_blocks(ids, parts, blocks, shards):
    groups, rows, width = parts.shape
    share = blocks * BLK // shards
    return pl.pallas_call(
        collect_kernel,
        in_specs=[SMEM_SPEC, VMEM_SPEC],
        out_specs=VMEM_SPEC,
        out_shape=jax.ShapeDtypeStruct((shards, share + rows - BLK, width), bf16),
        scratch_shapes=[pltpu.VMEM((blocks, BLK, width), f32)],
        name="collect_blocks",
    )(ids, parts)


def finish_kernel(parts_ref, machine_ref, *grad_refs):
    shards, rows, width = parts_ref.shape
    share = machine_ref.shape[0]
    lead = rows - share
    total = jnp.zeros((share, width), f32)
    for s in range(shards):
        total += parts_ref[s, 0:share, :].astype(f32)
        at = s * lead
        while at < (s + 1) * lead:
            which, row = at // width, at % width
            size = min((s + 1) * lead - at, width - row)
            start = share + at - s * lead
            grad_refs[which][row : row + size, :] = parts_ref[
                s, start : start + size, :
            ].astype(f32)
            at += size
    machine_ref[...] = total


def finish(parts, share):
    width = parts.shape[2]
    square = jax.ShapeDtypeStruct((width, width), f32)
    return pl.pallas_call(
        finish_kernel,
        in_specs=[VMEM_SPEC],
        out_specs=[VMEM_SPEC] * 4,
        out_shape=[jax.ShapeDtypeStruct((share, width), f32), square, square, square],
        name="finish",
    )(parts)


def swap(x, axis):
    return lax.all_to_all(x, axis, split_axis=0, concat_axis=0, tiled=True)


def per_device(op_embed, machine_embed, cotangent, w_query, w_key, w_value, slot_local, counts):
    groups = lax.axis_size("grp")
    shards = lax.axis_size("ops")
    width = op_embed.shape[1]
    machine_rows = machine_embed.shape[0]
    blocks_here = machine_rows // BLK
    ids = swap(slot_local.reshape(groups, 1), "grp")[:, 0]
    outgoing = pick_blocks(ids, machine_embed.reshape(blocks_here, BLK, width))
    rows = swap(outgoing, "grp")
    lead = 3 * width // shards
    back, op_grad, wgrad = attend(
        rows, counts.T, op_embed, cotangent, w_query, w_key, w_value, extra=lead
    )
    scattered = swap(wgrad.reshape(shards, lead, width), "ops")
    returned = swap(fill_tail(scattered, back), "grp")
    shares = swap(collect_blocks(ids, returned, blocks_here, shards), "ops")
    machine_grad, grad_wq, grad_wk, grad_wv = finish(shares, machine_rows // shards)
    return (op_grad, machine_grad, grad_wq, grad_wk, grad_wv)


def solution(mesh):
    return jax.shard_map(
        per_device,
        mesh=mesh,
        in_specs=(
            P(("grp", "ops"), None),
            P("grp", None),
            P(("grp", "ops"), None),
            P(),
            P(),
            P(),
            P(("grp", "ops"), None),
            P(("grp", "ops"), None),
        ),
        out_specs=(P(("grp", "ops"), None), P(("grp", "ops"), None), P(), P(), P()),
        check_vma=False,
    )
```

time: 189 us -> 173 us (0.915); the launches traced: 186 us -> 173 us
  blocking collectives: 56.2 us -> 105 us
  waiting for transfers between devices: 74.7 us -> 26.7 us
  starting transfers between devices: 18.3 us -> 4.24 us
  Pallas kernels: 28.9 us -> 32.7 us
  other arithmetic: 2.89 us -> 0.89 us
    all_to_all x3 -> x4, blocking collectives: 56.2 us -> 105 us  [swap(): return lax.all_to_all(x, axis, split_axis=0, concat_axis=0, tiled=True)]
    all_to_all x4 -> x1, waiting for transfers between devices: 74.7 us -> 26.7 us  [swap(): return lax.all_to_all(x, axis, split_axis=0, concat_axis=0, tiled=True)]
    all_to_all x4 -> x1, starting transfers between devices: 18.3 us -> 4.24 us  [swap(): return lax.all_to_all(x, axis, split_axis=0, concat_axis=0, tiled=True)]
    pallas_call x1 -> x3, Pallas kernels: 24.7 us -> 28.3 us  [the longest x1 24.4 us: attend(): pl.pallas_call(attend_kernel, in_specs=[VMEM_SPEC] * 8, out_specs=[VMEM_S...]
  transfers between devices with their start and end apart: 4 -> 1, of which waited for: 4 -> 1; matrix products, arithmetic and copies ran while one was open for 1% -> 1% of each run, Pallas kernels for 1% -> 0%
where the time goes in v2:
time: 173 us
  blocking collectives  105 us (61%)
  Pallas kernels  32.7 us (19%)
  waiting for transfers between devices  26.7 us (15%)
  starting transfers between devices  4.24 us (2%)
  local copies, waits for them, and re-layouts  3.1 us (2%)
    all_to_all x4, blocking collectives, swap(): return lax.all_to_all(x, axis, split_axis=0, concat_axis=0, tiled=True)  105 us
    all_to_all x1, waiting for transfers between devices, swap(): return lax.all_to_all(x, axis, split_axis=0, concat_axis=0, tiled=True)  26.7 us
    pallas_call x1, Pallas kernels, attend(): pl.pallas_call(attend_kernel, in_specs=[VMEM_SPEC] * 8, out_specs=[VMEM_S...  24.4 us
    all_to_all x1, starting transfers between devices, swap(): return lax.all_to_all(x, axis, split_axis=0, concat_axis=0, tiled=True)  4.24 us
  transfers between devices with their start and end apart: 1, of which 1 were waited for; matrix products, arithmetic and copies ran while one was open for 1% of the time, Pallas kernels for 0%

profile of v2, /device:TPU:1, one launch (start us, length us, event | category | flops | bytes accessed | tf_op | source)
XLA Modules:
  0.0 172.8 jit_solution(2051434745209794099)
XLA Ops:
  0.6 0.7 copy.17
  1.4 16.3 %all_to_all.29 = s32[16,1,1]{2,1,0:T(1,128)S(1)} all-to-all(s32[16,1,1]{2,1,0:T(1,128)S(1)} %copy.17), channel_id=1, replica_groups=mesh['grp'=16,'ops'=32] {'grp'}, dimensions={0} | all-to-all | bytes 128 | tf_op jit(solution)/shard_map/all_to_all | solution.py:253
  17.7 0.9 reduce.ids_ref
  18.6 2.0 %pick_blocks.1 = bf16[16,128,256]{2,1,0:T(8,128)(2,1)} custom-call(s32[16]{0:T(128)} %reduce.ids_ref, bf16[4,128,256]{2,1,0:T(8,128)(2,1)} %bitcast.7), custom_call_target="tpu_custom_call" | custom-call | tf_op jit(solution)/shard_map/pick_blocks/pallas_call | solution.py:147
  20.6 0.0 copy-start.2
  20.6 0.0 copy-start.1
  20.6 4.2 %all-to-all-start.1 = ((bf16[16,128,256]{2,1,0:T(8,128)(2,1)}), bf16[16,128,256]{2,1,0:T(8,128)(2,1)S(1)}, u32[]{:S(2)}, u32[]{:S(2)}) async-start(bf16[16,128,256]{2,1,0:T(8,128)(2,1)} %pick_blocks.1), calls=%async_computation.1 | async-start | bytes 2097152 | tf_op jit(solution)/shard_map/all_to_all | solution.py:253
  24.8 0.0 copy-done.2
  24.8 0.6 reshape.25.counts_ref
  25.4 0.0 copy-done.1
  25.4 0.8 copy.18
  26.2 26.7 %all-to-all-done.1.rows_ref = bf16[16,128,256]{2,1,0:T(8,128)(2,1)S(1)} async-done(((bf16[16,128,256]{2,1,0:T(8,128)(2,1)}), bf16[16,128,256]{2,1,0:T(8,128)(2,1)S(1)}, u32[]{:S(2)}, u32[]{:S(2)}) %all-to-all-start.1) | async-done | bytes 1048608 | tf_op jit(solution)/shard_map/all_to_all | solution.py:253
  52.8 0.0 copy-start
  52.8 1.0 copy-done
  53.8 24.4 %attend.1 = (bf16[16,152,256]{2,1,0:T(8,128)(2,1)}, bf16[256,256]{1,0:T(8,128)(2,1)}, bf16[768,256]{1,0:T(8,128)(2,1)}) custom-call(bf16[16,128,256]{2,1,0:T(8,128)(2,1)} %copy-done, s32[16,1,256]{2,1,0:T(1,128)} %reshape.25.counts_ref, bf16[256,256]{1,0:T(8,128)(2,1)} %op_ref.1, bf16[256,256]{1,0:T(8,128)(2,1)} %cot_ref.1, bf16[256,256]{1,0:T(8,128)(2,1)} %wq_ref.1, ...), custom_call_target="tpu_custom_call" | custom-call | tf_op jit(solution)/shard_map/attend/pallas_call | solution.py:113
  78.2 26.0 %all_to_all.30.parts_ref = bf16[32,24,256]{2,1,0:T(8,128)(2,1)} all-to-all(bf16[32,24,256]{2,1,0:T(8,128)(2,1)} %bitcast.6), channel_id=1, replica_groups=mesh['grp'=16,'ops'=32] {'ops'}, dimensions={0} | all-to-all | bytes 786432 | tf_op jit(solution)/shard_map/all_to_all | solution.py:253
  104.2 1.9 %fill_tail.1 = bf16[16,152,256]{2,1,0:T(8,128)(2,1)} custom-call(bf16[32,24,256]{2,1,0:T(8,128)(2,1)} %all_to_all.30.parts_ref, bf16[16,152,256]{2,1,0:T(8,128)(2,1)} %get-tuple-element.14.buffer_ref), custom_call_target="tpu_custom_call", output_to_operand_aliasing={{}: (1, {})} | custom-call | tf_op jit(solution)/shard_map/fill_tail/pallas_call | solution.py:174
  106.1 37.1 %all_to_all.31.parts_ref = bf16[16,152,256]{2,1,0:T(8,128)(2,1)} all-to-all(bf16[16,152,256]{2,1,0:T(8,128)(2,1)} %fill_tail.1), channel_id=1, replica_groups=mesh['grp'=16,'ops'=32] {'grp'}, dimensions={0} | all-to-all | bytes 2490368 | tf_op jit(solution)/shard_map/all_to_all | solution.py:253
  143.2 2.4 %collect_blocks.1 = bf16[32,40,256]{2,1,0:T(8,128)(2,1)} custom-call(s32[16]{0:T(128)} %reduce.ids_ref, bf16[16,152,256]{2,1,0:T(8,128)(2,1)} %all_to_all.31.parts_ref), custom_call_target="tpu_custom_call" | custom-call | tf_op jit(solution)/shard_map/collect_blocks/pallas_call | solution.py:211
  145.6 25.3 %all_to_all.32.parts_ref = bf16[32,40,256]{2,1,0:T(8,128)(2,1)} all-to-all(bf16[32,40,256]{2,1,0:T(8,128)(2,1)} %collect_blocks.1), channel_id=1, replica_groups=mesh['grp'=16,'ops'=32] {'ops'}, dimensions={0} | all-to-all | bytes 1310720 | tf_op jit(solution)/shard_map/all_to_all | solution.py:253
  170.9 2.0 %finish.1 = (f32[16,256]{1,0:T(8,128)}, f32[256,256]{1,0:T(8,128)}, f32[256,256]{1,0:T(8,128)}, f32[256,256]{1,0:T(8,128)}) custom-call(bf16[32,40,256]{2,1,0:T(8,128)(2,1)} %all_to_all.32.parts_ref), custom_call_target="tpu_custom_call" | custom-call | tf_op jit(solution)/shard_map/finish/pallas_call | solution.py:243
Async XLA Ops:
  20.6 4.2 %copy-start.2 = (s32[256,16]{0,1:T(8,128)S(1)}, s32[256,16]{0,1:T(8,128)}, u32[]{:S(2)}) copy-start(s32[256,16]{0,1:T(8,128)} %param.15) | copy-start | bytes 49156
  20.6 4.9 %copy-start.1 = (bf16[256,256]{1,0:T(8,128)(2,1)S(1)}, bf16[256,256]{1,0:T(8,128)(2,1)}, u32[]{:S(2)}) copy-start(bf16[256,256]{1,0:T(8,128)(2,1)} %wk_ref.1) | copy-start | bytes 393220
  20.6 32.3 %all-to-all-start.1 = ((bf16[16,128,256]{2,1,0:T(8,128)(2,1)}), bf16[16,128,256]{2,1,0:T(8,128)(2,1)S(1)}, u32[]{:S(2)}, u32[]{:S(2)}) async-start(bf16[16,128,256]{2,1,0:T(8,128)(2,1)} %pick_blocks.1), calls=%async_computation.1 | async-start | bytes 2097152 | tf_op jit(solution)/shard_map/all_to_all | solution.py:253
  52.8 1.0 copy-start

commit v3 on v2

v3 whole, which is shorter than its diff:
```python
import jax
import jax.numpy as jnp
from jax import lax
from jax.experimental import pallas as pl
from jax.experimental.pallas import tpu as pltpu
from jax.sharding import PartitionSpec as P


HEADS = 8
BLK = 128
X_SIZE = 4
Z_SIZE = 8
MEAN_SCALE = 0.08838834764831845

f32 = jnp.float32
bf16 = jnp.bfloat16
VMEM_SPEC = pl.BlockSpec(memory_space=pltpu.VMEM)
SMEM_SPEC = pl.BlockSpec(memory_space=pltpu.SMEM)


def dot(a, b):
    return jnp.dot(a, b, preferred_element_type=f32)


def dot_nt(a, b):
    return lax.dot_general(a, b, (((1,), (1,)), ((), ())), preferred_element_type=f32)


def dot_tt(a, b):
    return lax.dot_general(a, b, (((0,), (1,)), ((), ())), preferred_element_type=f32)


def dot_tn(a, b):
    return lax.dot_general(a, b, (((0,), (0,)), ((), ())), preferred_element_type=f32)


def attend_kernel(
    place_ref,
    rows_ref,
    counts_ref,
    op_ref,
    cot_ref,
    wq_ref,
    wk_ref,
    wv_ref,
    wkt_ref,
    back_ref,
    opg_ref,
    own_ref,
    *rest,
):
    send_refs, (qm_ref, cm_ref, gq_ref, wkv_ref, ct_ref, wgrad_ref) = rest[:-6], rest[-6:]
    slots, blk, width = rows_ref.shape
    ops_count = op_ref.shape[0]
    head_size = width // HEADS
    inv_root = head_size ** (-0.5)
    d_scale = 0.25 * MEAN_SCALE * inv_root
    pair = 8
    machines = pair * blk

    queries = dot(op_ref[...], wq_ref[...]).astype(bf16)
    cot = cot_ref[...]
    ct_ref[...] = cot.T
    lane_head = lax.broadcasted_iota(jnp.int32, (ops_count, width), 1) // head_size
    zero = jnp.zeros((), bf16)
    for h in range(HEADS):
        here = lane_head == h
        qm_ref[pl.ds(h * ops_count, ops_count), :] = jnp.where(here, queries, zero)
        cm_ref[pl.ds(h * ops_count, ops_count), :] = jnp.where(here, cot, zero)
    gq_ref[...] = jnp.zeros_like(gq_ref)
    wkv_ref[...] = jnp.zeros_like(wkv_ref)

    def one_pair(step, carry):
        first = step * pair
        embed = rows_ref[pl.ds(first, pair)].reshape(machines, width)
        keys = dot(embed, wk_ref[...]).astype(bf16)
        values = dot(embed, wv_ref[...]).astype(bf16)
        keys_t = keys.T
        place = lax.broadcasted_iota(jnp.int32, (blk, ops_count), 0)
        eligible = jnp.concatenate(
            [place < counts_ref[first + s] for s in range(pair)], axis=0
        )
        key_grad = jnp.zeros((machines, width), f32)
        value_grad = []
        for h in range(HEADS):
            q_h = qm_ref[pl.ds(h * ops_count, ops_count), :]
            c_h = cm_ref[pl.ds(h * ops_count, ops_count), :]
            scores = dot_nt(keys, q_h)
            value_dot = dot_nt(values, c_h)
            half = jnp.tanh(scores * (0.5 * inv_root))
            gate2 = jnp.where(eligible, 1.0 + half, 0.0).astype(bf16)
            slope = jnp.where(eligible, value_dot * (1.0 - half * half), 0.0).astype(bf16)
            key_grad += dot(slope, q_h)
            value_grad.append(dot_nt(ct_ref[h * head_size : (h + 1) * head_size, :], gate2))
            gq_ref[pl.ds(h * head_size, head_size), :] += dot(
                keys_t[h * head_size : (h + 1) * head_size, :], slope
            )
        key_grad = (key_grad * d_scale).astype(bf16)
        value_grad = (jnp.concatenate(value_grad, axis=0) * (0.5 * MEAN_SCALE)).astype(bf16)
        back = dot_nt(key_grad, wk_ref[...]) + dot_tt(value_grad, wv_ref[...])
        back = back.astype(bf16)
        for s in range(pair):
            back_ref[first + s, 0:blk, :] = back[s * blk : (s + 1) * blk]
        wkv_ref[0:width, :] += dot_tn(embed, key_grad)
        wkv_ref[width : 2 * width, :] += dot(value_grad, embed)
        return carry

    lax.fori_loop(0, slots // pair, one_pair, 0)
    grad_query = (gq_ref[...] * d_scale).T.astype(bf16)
    opg_ref[...] = (cot.astype(f32) + dot_nt(grad_query, wq_ref[...])).astype(bf16)
    wgrad_ref[0:width, :] = dot_tn(op_ref[...], grad_query)
    wgrad_ref[width : 2 * width, :] = wkv_ref[0:width, :]
    wgrad_ref[2 * width : 3 * width, :] = wkv_ref[width : 2 * width, :].T
    part = own_ref.shape[0]
    own_ref[...] = wgrad_ref[pl.ds(pl.multiple_of(place_ref[0] * part, 8), part), :]
    for d, send_ref in enumerate(send_refs):
        other = lax.rem(place_ref[0] + d + 1, len(send_refs) + 1)
        send_ref[...] = wgrad_ref[pl.ds(pl.multiple_of(other * part, 8), part), :].astype(bf16)


def attend(place, rows, counts_t, op_embed, cotangent, w_query, w_key, w_value):
    slots, blk, width = rows.shape
    ops_count = op_embed.shape[0]
    part = 3 * width // X_SIZE
    return pl.pallas_call(
        attend_kernel,
        in_specs=[SMEM_SPEC] + [VMEM_SPEC] * 8,
        out_specs=[VMEM_SPEC] * (2 + X_SIZE),
        out_shape=[
            jax.ShapeDtypeStruct((slots, blk, width), bf16),
            jax.ShapeDtypeStruct((ops_count, width), bf16),
            jax.ShapeDtypeStruct((part, width), f32),
        ]
        + [jax.ShapeDtypeStruct((part, width), bf16)] * (X_SIZE - 1),
        scratch_shapes=[
            pltpu.VMEM((HEADS * ops_count, width), bf16),
            pltpu.VMEM((HEADS * ops_count, width), bf16),
            pltpu.VMEM((width, ops_count), f32),
            pltpu.VMEM((2 * width, width), f32),
            pltpu.VMEM((width, ops_count), bf16),
            pltpu.VMEM((3 * width, width), f32),
        ],
        name="attend",
    )(
        place,
        rows,
        counts_t.reshape(slots, 1, ops_count),
        op_embed,
        cotangent,
        w_query,
        w_key,
        w_value,
        w_key.T,
    )


def fold_kernel(place_ref, own_ref, *refs):
    got, own_out, sends, total_ref = (
        refs[: X_SIZE - 1],
        refs[X_SIZE - 1],
        refs[X_SIZE:-1],
        refs[-1],
    )
    total = own_ref[...]
    for ref in got:
        total += ref[...].astype(f32)
    total_ref[...] = total
    part = own_out.shape[0]
    own_out[...] = total_ref[pl.ds(pl.multiple_of(place_ref[1] * part, 8), part), :]
    for d, send_ref in enumerate(sends):
        other = lax.rem(place_ref[1] + d + 1, Z_SIZE)
        send_ref[...] = total_ref[pl.ds(pl.multiple_of(other * part, 8), part), :]


def fold(place, own, got):
    rows, width = own.shape
    piece = jax.ShapeDtypeStruct((rows // Z_SIZE, width), f32)
    return pl.pallas_call(
        fold_kernel,
        in_specs=[SMEM_SPEC] + [VMEM_SPEC] * X_SIZE,
        out_specs=[VMEM_SPEC] * Z_SIZE,
        out_shape=[piece] * Z_SIZE,
        scratch_shapes=[pltpu.VMEM(own.shape, f32)],
        name="fold",
    )(place, own, *got)


def spread_kernel(*refs):
    out_ref = refs[-1]
    total = refs[0][...]
    for ref in refs[1:-1]:
        total += ref[...]
    total = total.astype(bf16)
    for g in range(out_ref.shape[0]):
        out_ref[g] = total


def spread(pieces, groups):
    return pl.pallas_call(
        spread_kernel,
        in_specs=[VMEM_SPEC] * len(pieces),
        out_specs=VMEM_SPEC,
        out_shape=jax.ShapeDtypeStruct((groups,) + pieces[0].shape, bf16),
        name="spread",
    )(*pieces)


def pick_kernel(ids_ref, blocks_ref, out_ref):
    for g in range(out_ref.shape[0]):
        out_ref[g] = blocks_ref[ids_ref[g]]


def pick_blocks(ids, blocks):
    return pl.pallas_call(
        pick_kernel,
        in_specs=[SMEM_SPEC, VMEM_SPEC],
        out_specs=VMEM_SPEC,
        out_shape=jax.ShapeDtypeStruct((ids.shape[0],) + blocks.shape[1:], blocks.dtype),
        name="pick_blocks",
    )(ids, blocks)


def collect_kernel(ids_ref, parts_ref, lead_ref, out_ref, acc_ref):
    shards, rows, width = out_ref.shape
    blocks, blk, _ = acc_ref.shape
    share = blocks * blk // shards
    lead = rows - share
    groups = parts_ref.shape[0]
    acc_ref[...] = jnp.zeros_like(acc_ref)
    total = jnp.zeros((lead, width), f32)
    for g in range(groups):
        acc_ref[ids_ref[g]] += parts_ref[g].astype(f32)
        total += lead_ref[g].astype(f32)
    total = (total * (1.0 / (groups * shards))).astype(bf16)
    for s in range(shards):
        at = s * share
        out_ref[s, 0:share, :] = acc_ref[at // blk, at % blk : at % blk + share, :].astype(
            bf16
        )
        out_ref[s, share:rows, :] = total


def collect_blocks(ids, parts, leads, blocks, shards):
    width = parts.shape[2]
    rows = blocks * BLK // shards + leads.shape[1]
    return pl.pallas_call(
        collect_kernel,
        in_specs=[SMEM_SPEC, VMEM_SPEC, VMEM_SPEC],
        out_specs=VMEM_SPEC,
        out_shape=jax.ShapeDtypeStruct((shards, rows, width), bf16),
        scratch_shapes=[pltpu.VMEM((blocks, BLK, width), f32)],
        name="collect_blocks",
    )(ids, parts, leads)


def finish_kernel(parts_ref, machine_ref, *grad_refs):
    shards, rows, width = parts_ref.shape
    share = machine_ref.shape[0]
    lead = rows - share
    total = jnp.zeros((share, width), f32)
    for s in range(shards):
        total += parts_ref[s, 0:share, :].astype(f32)
        at = s * lead
        while at < (s + 1) * lead:
            which, row = at // width, at % width
            size = min((s + 1) * lead - at, width - row)
            start = share + at - s * lead
            grad_refs[which][row : row + size, :] = parts_ref[
                s, start : start + size, :
            ].astype(f32)
            at += size
    machine_ref[...] = total


def finish(parts, share):
    width = parts.shape[2]
    square = jax.ShapeDtypeStruct((width, width), f32)
    return pl.pallas_call(
        finish_kernel,
        in_specs=[VMEM_SPEC],
        out_specs=[VMEM_SPEC] * 4,
        out_shape=[jax.ShapeDtypeStruct((share, width), f32), square, square, square],
        name="finish",
    )(parts)


def swap(x, axis):
    return lax.all_to_all(x, axis, split_axis=0, concat_axis=0, tiled=True)


def shift_x(x, d):
    pairs = [
        (i * Z_SIZE + k, (i + d) % X_SIZE * Z_SIZE + k)
        for i in range(X_SIZE)
        for k in range(Z_SIZE)
    ]
    return lax.ppermute(x, "ops", pairs)


def shift_z(x, d):
    pairs = [
        (i * Z_SIZE + k, i * Z_SIZE + (k + d) % Z_SIZE)
        for i in range(X_SIZE)
        for k in range(Z_SIZE)
    ]
    return lax.ppermute(x, "ops", pairs)


def per_device(op_embed, machine_embed, cotangent, w_query, w_key, w_value, slot_local, counts):
    groups = lax.axis_size("grp")
    shards = lax.axis_size("ops")
    width = op_embed.shape[1]
    machine_rows = machine_embed.shape[0]
    blocks_here = machine_rows // BLK
    ids = swap(slot_local.reshape(groups, 1), "grp")[:, 0]
    outgoing = pick_blocks(ids, machine_embed.reshape(blocks_here, BLK, width))
    rows = swap(outgoing, "grp")
    spot = lax.axis_index("ops")
    place = jnp.stack([spot // Z_SIZE, spot % Z_SIZE]).astype(jnp.int32)
    back, op_grad, own, *sends = attend(
        place, rows, counts.T, op_embed, cotangent, w_query, w_key, w_value
    )
    returned = swap(back, "grp")
    got = [shift_x(send, d + 1) for d, send in enumerate(sends)]
    own, *sends = fold(place, own, got)
    got = [shift_z(send, d + 1) for d, send in enumerate(sends)]
    leads = spread([own] + got, groups)
    leads = swap(leads, "grp")
    shares = swap(collect_blocks(ids, returned, leads, blocks_here, shards), "ops")
    machine_grad, grad_wq, grad_wk, grad_wv = finish(shares, machine_rows // shards)
    return (op_grad, machine_grad, grad_wq, grad_wk, grad_wv)


def solution(mesh):
    return jax.shard_map(
        per_device,
        mesh=mesh,
        in_specs=(
            P(("grp", "ops"), None),
            P("grp", None),
            P(("grp", "ops"), None),
            P(),
            P(),
            P(),
            P(("grp", "ops"), None),
            P(("grp", "ops"), None),
        ),
        out_specs=(P(("grp", "ops"), None), P(("grp", "ops"), None), P(), P(), P()),
        check_vma=False,
    )
```

time: 173 us -> 200 us (1.16)
  starting transfers between devices: 4.24 us -> 45.6 us
  blocking collectives: 105 us -> 89.8 us
  Pallas kernels: 32.7 us -> 24.7 us
  waiting for transfers between devices: 26.7 us -> 31.4 us
    ppermute x0 -> x10, starting transfers between devices: none -> 41.4 us  [the longest x7 31.6 us: shift_z(): return lax.ppermute(x, 'ops', pairs)]
    all_to_all x4, blocking collectives: 105 us -> 89.8 us  [swap(): return lax.all_to_all(x, axis, split_axis=0, concat_axis=0, tiled=True)]
    pallas_call x3 -> x4, Pallas kernels: 28.7 us -> 20.7 us  [the longest x1 14.9 us: attend(): pl.pallas_call(attend_kernel, in_specs=[SMEM_SPEC] + [VMEM_SPEC] * 8, out...]
    ppermute x0 -> x10, waiting for transfers between devices: none -> 6.02 us  [the longest x3 3.21 us: shift_x(): return lax.ppermute(x, 'ops', pairs)]
    unnamed x7 -> x31, local copies, waits for them, and re-layouts: 1.75 us -> 4.28 us
  transfers between devices with their start and end apart: 1 -> 11, of which waited for: 1 -> 4; matrix products, arithmetic and copies ran while one was open for 1% -> 1% of each run, Pallas kernels for 0% -> 0%
where the time goes in v3:
time: 200 us; the launch traced here: 199 us
  blocking collectives  89.8 us (45%)
  starting transfers between devices  45.6 us (23%)
  waiting for transfers between devices  31.4 us (16%)
  Pallas kernels  24.7 us (12%)
  local copies, waits for them, and re-layouts  4.98 us (2%)
    all_to_all x4, blocking collectives, swap(): return lax.all_to_all(x, axis, split_axis=0, concat_axis=0, tiled=True)  89.8 us
    ppermute x7, starting transfers between devices, shift_z(): return lax.ppermute(x, 'ops', pairs)  31.6 us
    all_to_all x1, waiting for transfers between devices, swap(): return lax.all_to_all(x, axis, split_axis=0, concat_axis=0, tiled=True)  25.4 us
    pallas_call x1, Pallas kernels, attend(): pl.pallas_call(attend_kernel, in_specs=[SMEM_SPEC] + [VMEM_SPEC] * 8, out...  14.9 us
    ppermute x3, starting transfers between devices, shift_x(): return lax.ppermute(x, 'ops', pairs)  9.78 us
    unnamed x31, local copies, waits for them, and re-layouts  4.28 us
    all_to_all x1, starting transfers between devices, swap(): return lax.all_to_all(x, axis, split_axis=0, concat_axis=0, tiled=True)  4.24 us
  transfers between devices with their start and end apart: 11, of which 4 were waited for; matrix products, arithmetic and copies ran while one was open for 1% of the time, Pallas kernels for 0%

profile of v3, /device:TPU:1, one launch (start us, length us, event | category | flops | bytes accessed | tf_op | source)
XLA Modules:
  0.0 198.9 jit_solution(17252463874363245983)
XLA Ops:
  1.4 16.3 %all_to_all.29 = s32[16,1,1]{2,1,0:T(1,128)S(1)} all-to-all(s32[16,1,1]{2,1,0:T(1,128)S(1)} %copy.16), channel_id=1, replica_groups=mesh['grp'=16,'ops'=32] {'grp'}, dimensions={0} | all-to-all | bytes 128 | tf_op jit(solution)/shard_map/all_to_all | solution.py:288
  18.6 2.0 %pick_blocks.1 = bf16[16,128,256]{2,1,0:T(8,128)(2,1)} custom-call(s32[16]{0:T(128)} %reduce.ids_ref, bf16[4,128,256]{2,1,0:T(8,128)(2,1)} %bitcast.7), custom_call_target="tpu_custom_call" | custom-call | tf_op jit(solution)/shard_map/pick_blocks/pallas_call | solution.py:214
  20.7 4.2 %all-to-all-start.1 = ((bf16[16,128,256]{2,1,0:T(8,128)(2,1)}), bf16[16,128,256]{2,1,0:T(8,128)(2,1)S(1)}, u32[]{:S(2)}, u32[]{:S(2)}) async-start(bf16[16,128,256]{2,1,0:T(8,128)(2,1)} %pick_blocks.1), calls=%async_computation.1 | async-start | bytes 2097152 | tf_op jit(solution)/shard_map/all_to_all | solution.py:288
  27.6 25.4 %all-to-all-done.1.rows_ref = bf16[16,128,256]{2,1,0:T(8,128)(2,1)S(1)} async-done(((bf16[16,128,256]{2,1,0:T(8,128)(2,1)}), bf16[16,128,256]{2,1,0:T(8,128)(2,1)S(1)}, u32[]{:S(2)}, u32[]{:S(2)}) %all-to-all-start.1) | async-done | bytes 1048608 | tf_op jit(solution)/shard_map/all_to_all | solution.py:288
  53.9 14.9 %attend.1 = (bf16[16,128,256]{2,1,0:T(8,128)(2,1)}, bf16[256,256]{1,0:T(8,128)(2,1)}, f32[192,256]{1,0:T(8,128)}, bf16[192,256]{1,0:T(8,128)(2,1)}, bf16[192,256]{1,0:T(8,128)(2,1)}, /*index=5*/bf16[192,256]{1,0:T(8,128)(2,1)}) custom-call(s32[2]{0:T(128)} %pad_add_fusion.place_ref, bf16[16,128,256]{2,1,0:T(8,128)(2,1)} %copy-done, ...), custom_call_target="tpu_custom_call" | custom-call | tf_op jit(solution)/shard_map/attend/pallas_call | solution.py:125
  68.8 2.4 %collective-permute-start = (bf16[192,256]{1,0:T(8,128)(2,1)}, bf16[192,256]{1,0:T(8,128)(2,1)S(1)}, u32[]{:S(2)}, u32[]{:S(2)}) collective-permute-start(bf16[192,256]{1,0:T(8,128)(2,1)} %get-tuple-element.26), channel_id=1, source_target_pairs={{0,8},{1,9},{2,10},{3,11},{4,12},{5,13},{6,14},{7,15},{8,16},{9,17... | collective-permute-start | bytes 294920 | tf_op jit(solution)/shard_map/ppermute | solution.py:297
  71.2 4.4 %collective-permute-start.1 = (bf16[192,256]{1,0:T(8,128)(2,1)}, bf16[192,256]{1,0:T(8,128)(2,1)S(1)}, u32[]{:S(2)}, u32[]{:S(2)}) collective-permute-start(bf16[192,256]{1,0:T(8,128)(2,1)} %get-tuple-element.27), channel_id=1, source_target_pairs={{0,16},{1,17},{2,18},{3,19},{4,20},{5,21},{6,22},{7,23},{8,24},{9,... | collective-permute-start | bytes 294920 | tf_op jit(solution)/shard_map/ppermute | solution.py:297
  75.6 3.1 %collective-permute-start.2 = (bf16[192,256]{1,0:T(8,128)(2,1)}, bf16[192,256]{1,0:T(8,128)(2,1)S(1)}, u32[]{:S(2)}, u32[]{:S(2)}) collective-permute-start(bf16[192,256]{1,0:T(8,128)(2,1)} %get-tuple-element.28), channel_id=1, source_target_pairs={{0,24},{1,25},{2,26},{3,27},{4,28},{5,29},{6,30},{7,31},{8,0},{9,1... | collective-permute-start | bytes 294920 | tf_op jit(solution)/shard_map/ppermute | solution.py:297
  78.7 3.1 %collective-permute-done.2.refs_2_ = bf16[192,256]{1,0:T(8,128)(2,1)S(1)} collective-permute-done((bf16[192,256]{1,0:T(8,128)(2,1)}, bf16[192,256]{1,0:T(8,128)(2,1)S(1)}, u32[]{:S(2)}, u32[]{:S(2)}) %collective-permute-start.2) | collective-permute-done | bytes 98336 | tf_op jit(solution)/shard_map/ppermute | solution.py:297
  82.5 1.8 fold.1
  84.3 4.0 %collective-permute-start.3 = (f32[24,256]{1,0:T(8,128)}, f32[24,256]{1,0:T(8,128)S(1)}, u32[]{:S(2)}, u32[]{:S(2)}) collective-permute-start(f32[24,256]{1,0:T(8,128)} %get-tuple-element.30), channel_id=1, source_target_pairs={{0,1},{1,2},{2,3},{3,4},{4,5},{5,6},{6,7},{7,0},{8,9},{9,10},{10,1... | collective-permute-start | bytes 73736 | tf_op jit(solution)/shard_map/ppermute | solution.py:306
  88.3 5.8 %collective-permute-start.4 = (f32[24,256]{1,0:T(8,128)}, f32[24,256]{1,0:T(8,128)S(1)}, u32[]{:S(2)}, u32[]{:S(2)}) collective-permute-start(f32[24,256]{1,0:T(8,128)} %get-tuple-element.31), channel_id=1, source_target_pairs={{0,2},{1,3},{2,4},{3,5},{4,6},{5,7},{6,0},{7,1},{8,10},{9,11},{10,... | collective-permute-start | bytes 73736 | tf_op jit(solution)/shard_map/ppermute | solution.py:306
  94.1 7.0 %collective-permute-start.5 = (f32[24,256]{1,0:T(8,128)}, f32[24,256]{1,0:T(8,128)S(1)}, u32[]{:S(2)}, u32[]{:S(2)}) collective-permute-start(f32[24,256]{1,0:T(8,128)} %get-tuple-element.32), channel_id=1, source_target_pairs={{0,3},{1,4},{2,5},{3,6},{4,7},{5,0},{6,1},{7,2},{8,11},{9,12},{10,... | collective-permute-start | bytes 73736 | tf_op jit(solution)/shard_map/ppermute | solution.py:306
  101.2 2.8 %collective-permute-start.6 = (f32[24,256]{1,0:T(8,128)}, f32[24,256]{1,0:T(8,128)S(1)}, u32[]{:S(2)}, u32[]{:S(2)}) collective-permute-start(f32[24,256]{1,0:T(8,128)} %get-tuple-element.33), channel_id=1, source_target_pairs={{0,4},{1,5},{2,6},{3,7},{4,0},{5,1},{6,2},{7,3},{8,12},{9,13},{10,... | collective-permute-start | bytes 73736 | tf_op jit(solution)/shard_map/ppermute | solution.py:306
  104.0 6.4 %collective-permute-start.7 = (f32[24,256]{1,0:T(8,128)}, f32[24,256]{1,0:T(8,128)S(1)}, u32[]{:S(2)}, u32[]{:S(2)}) collective-permute-start(f32[24,256]{1,0:T(8,128)} %get-tuple-element.34), channel_id=1, source_target_pairs={{0,5},{1,6},{2,7},{3,0},{4,1},{5,2},{6,3},{7,4},{8,13},{9,14},{10,... | collective-permute-start | bytes 73736 | tf_op jit(solution)/shard_map/ppermute | solution.py:306
  110.4 3.4 %collective-permute-start.8 = (f32[24,256]{1,0:T(8,128)}, f32[24,256]{1,0:T(8,128)S(1)}, u32[]{:S(2)}, u32[]{:S(2)}) collective-permute-start(f32[24,256]{1,0:T(8,128)} %get-tuple-element.35), channel_id=1, source_target_pairs={{0,6},{1,7},{2,0},{3,1},{4,2},{5,3},{6,4},{7,5},{8,14},{9,15},{10,... | collective-permute-start | bytes 73736 | tf_op jit(solution)/shard_map/ppermute | solution.py:306
  113.8 2.2 %collective-permute-start.9 = (f32[24,256]{1,0:T(8,128)}, f32[24,256]{1,0:T(8,128)S(1)}, u32[]{:S(2)}, u32[]{:S(2)}) collective-permute-start(f32[24,256]{1,0:T(8,128)} %get-tuple-element.36), channel_id=1, source_target_pairs={{0,7},{1,0},{2,1},{3,2},{4,3},{5,4},{6,5},{7,6},{8,15},{9,8},{10,9... | collective-permute-start | bytes 73736 | tf_op jit(solution)/shard_map/ppermute | solution.py:306
  116.1 2.8 %collective-permute-done.9.refs_7_ = f32[24,256]{1,0:T(8,128)S(1)} collective-permute-done((f32[24,256]{1,0:T(8,128)}, f32[24,256]{1,0:T(8,128)S(1)}, u32[]{:S(2)}, u32[]{:S(2)}) %collective-permute-start.9) | collective-permute-done | bytes 24608 | tf_op jit(solution)/shard_map/ppermute | solution.py:306
  119.5 1.6 spread.1
  121.0 17.3 %all_to_all.30.lead_ref = bf16[16,24,256]{2,1,0:T(8,128)(2,1)} all-to-all(bf16[16,24,256]{2,1,0:T(8,128)(2,1)} %spread.1), channel_id=1, replica_groups=mesh['grp'=16,'ops'=32] {'grp'}, dimensions={0} | all-to-all | bytes 393216 | tf_op jit(solution)/shard_map/all_to_all | solution.py:288
  138.3 31.4 %all_to_all.31.parts_ref = bf16[16,128,256]{2,1,0:T(8,128)(2,1)} all-to-all(bf16[16,128,256]{2,1,0:T(8,128)(2,1)S(1)} %copy-done.1), channel_id=1, replica_groups=mesh['grp'=16,'ops'=32] {'grp'}, dimensions={0} | all-to-all | bytes 2097152 | tf_op jit(solution)/shard_map/all_to_all | solution.py:288
  169.8 2.4 %collect_blocks.1 = bf16[32,40,256]{2,1,0:T(8,128)(2,1)} custom-call(s32[16]{0:T(128)} %reduce.ids_ref, bf16[16,128,256]{2,1,0:T(8,128)(2,1)} %all_to_all.31.parts_ref, bf16[16,24,256]{2,1,0:T(8,128)(2,1)} %all_to_all.30.lead_ref), custom_call_target="tpu_custom_call" | custom-call | tf_op jit(solution)/shard_map/collect_blocks/pallas_call | solution.py:246
  172.1 24.8 %all_to_all.32.parts_ref = bf16[32,40,256]{2,1,0:T(8,128)(2,1)} all-to-all(bf16[32,40,256]{2,1,0:T(8,128)(2,1)} %collect_blocks.1), channel_id=1, replica_groups=mesh['grp'=16,'ops'=32] {'ops'}, dimensions={0} | all-to-all | bytes 1310720 | tf_op jit(solution)/shard_map/all_to_all | solution.py:288
  196.9 2.0 finish.1
  (43 shorter events, 6.6 us)
Async XLA Ops:
  0.6 0.7 copy-start.14
  20.7 5.6 %copy-start.2 = (bf16[256,256]{1,0:T(8,128)(2,1)S(1)}, bf16[256,256]{1,0:T(8,128)(2,1)}, u32[]{:S(2)}) copy-start(bf16[256,256]{1,0:T(8,128)(2,1)} %wk_ref.1) | copy-start | bytes 393220
  20.7 32.3 %all-to-all-start.1 = ((bf16[16,128,256]{2,1,0:T(8,128)(2,1)}), bf16[16,128,256]{2,1,0:T(8,128)(2,1)S(1)}, u32[]{:S(2)}, u32[]{:S(2)}) async-start(bf16[16,128,256]{2,1,0:T(8,128)(2,1)} %pick_blocks.1), calls=%async_computation.1 | async-start | bytes 2097152 | tf_op jit(solution)/shard_map/all_to_all | solution.py:288
  24.9 0.7 copy-start.13
  53.0 0.9 copy-start
  68.8 69.5 %copy-start.1 = (bf16[16,128,256]{2,1,0:T(8,128)(2,1)S(1)}, bf16[16,128,256]{2,1,0:T(8,128)(2,1)}, u32[]{:S(2)}) copy-start(bf16[16,128,256]{2,1,0:T(8,128)(2,1)} %get-tuple-element.24) | copy-start | bytes 3145732
  68.8 9.8 %collective-permute-start = (bf16[192,256]{1,0:T(8,128)(2,1)}, bf16[192,256]{1,0:T(8,128)(2,1)S(1)}, u32[]{:S(2)}, u32[]{:S(2)}) collective-permute-start(bf16[192,256]{1,0:T(8,128)(2,1)} %get-tuple-element.26), channel_id=1, source_target_pairs={{0,8},{1,9},{2,10},{3,11},{4,12},{5,13},{6,14},{7,15},{8,16},{9,17... | collective-permute-start | bytes 294920 | tf_op jit(solution)/shard_map/ppermute | solution.py:297
  71.2 7.5 %collective-permute-start.1 = (bf16[192,256]{1,0:T(8,128)(2,1)}, bf16[192,256]{1,0:T(8,128)(2,1)S(1)}, u32[]{:S(2)}, u32[]{:S(2)}) collective-permute-start(bf16[192,256]{1,0:T(8,128)(2,1)} %get-tuple-element.27), channel_id=1, source_target_pairs={{0,16},{1,17},{2,18},{3,19},{4,20},{5,21},{6,22},{7,23},{8,24},{9,... | collective-permute-start | bytes 294920 | tf_op jit(solution)/shard_map/ppermute | solution.py:297
  75.6 6.3 %collective-permute-start.2 = (bf16[192,256]{1,0:T(8,128)(2,1)}, bf16[192,256]{1,0:T(8,128)(2,1)S(1)}, u32[]{:S(2)}, u32[]{:S(2)}) collective-permute-start(bf16[192,256]{1,0:T(8,128)(2,1)} %get-tuple-element.28), channel_id=1, source_target_pairs={{0,24},{1,25},{2,26},{3,27},{4,28},{5,29},{6,30},{7,31},{8,0},{9,1... | collective-permute-start | bytes 294920 | tf_op jit(solution)/shard_map/ppermute | solution.py:297
  78.7 3.2 %copy-start.3 = (bf16[192,256]{1,0:T(8,128)(2,1)}, bf16[192,256]{1,0:T(8,128)(2,1)S(1)}, u32[]{:S(2)}) copy-start(bf16[192,256]{1,0:T(8,128)(2,1)S(1)} %collective-permute-done.refs_0_) | copy-start | bytes 294916
  78.7 3.2 %copy-start.4 = (bf16[192,256]{1,0:T(8,128)(2,1)}, bf16[192,256]{1,0:T(8,128)(2,1)S(1)}, u32[]{:S(2)}) copy-start(bf16[192,256]{1,0:T(8,128)(2,1)S(1)} %collective-permute-done.1.refs_1_) | copy-start | bytes 294916
  84.3 26.1 %collective-permute-start.3 = (f32[24,256]{1,0:T(8,128)}, f32[24,256]{1,0:T(8,128)S(1)}, u32[]{:S(2)}, u32[]{:S(2)}) collective-permute-start(f32[24,256]{1,0:T(8,128)} %get-tuple-element.30), channel_id=1, source_target_pairs={{0,1},{1,2},{2,3},{3,4},{4,5},{5,6},{6,7},{7,0},{8,9},{9,10},{10,1... | collective-permute-start | bytes 73736 | tf_op jit(solution)/shard_map/ppermute | solution.py:306
  88.3 25.5 %collective-permute-start.4 = (f32[24,256]{1,0:T(8,128)}, f32[24,256]{1,0:T(8,128)S(1)}, u32[]{:S(2)}, u32[]{:S(2)}) collective-permute-start(f32[24,256]{1,0:T(8,128)} %get-tuple-element.31), channel_id=1, source_target_pairs={{0,2},{1,3},{2,4},{3,5},{4,6},{5,7},{6,0},{7,1},{8,10},{9,11},{10,... | collective-permute-start | bytes 73736 | tf_op jit(solution)/shard_map/ppermute | solution.py:306
  94.1 21.9 %collective-permute-start.5 = (f32[24,256]{1,0:T(8,128)}, f32[24,256]{1,0:T(8,128)S(1)}, u32[]{:S(2)}, u32[]{:S(2)}) collective-permute-start(f32[24,256]{1,0:T(8,128)} %get-tuple-element.32), channel_id=1, source_target_pairs={{0,3},{1,4},{2,5},{3,6},{4,7},{5,0},{6,1},{7,2},{8,11},{9,12},{10,... | collective-permute-start | bytes 73736 | tf_op jit(solution)/shard_map/ppermute | solution.py:306
  101.2 14.9 %collective-permute-start.6 = (f32[24,256]{1,0:T(8,128)}, f32[24,256]{1,0:T(8,128)S(1)}, u32[]{:S(2)}, u32[]{:S(2)}) collective-permute-start(f32[24,256]{1,0:T(8,128)} %get-tuple-element.33), channel_id=1, source_target_pairs={{0,4},{1,5},{2,6},{3,7},{4,0},{5,1},{6,2},{7,3},{8,12},{9,13},{10,... | collective-permute-start | bytes 73736 | tf_op jit(solution)/shard_map/ppermute | solution.py:306
  104.0 12.0 %collective-permute-start.7 = (f32[24,256]{1,0:T(8,128)}, f32[24,256]{1,0:T(8,128)S(1)}, u32[]{:S(2)}, u32[]{:S(2)}) collective-permute-start(f32[24,256]{1,0:T(8,128)} %get-tuple-element.34), channel_id=1, source_target_pairs={{0,5},{1,6},{2,7},{3,0},{4,1},{5,2},{6,3},{7,4},{8,13},{9,14},{10,... | collective-permute-start | bytes 73736 | tf_op jit(solution)/shard_map/ppermute | solution.py:306
  110.4 8.5 %copy-start.6 = (f32[24,256]{1,0:T(8,128)}, f32[24,256]{1,0:T(8,128)S(1)}, u32[]{:S(2)}) copy-start(f32[24,256]{1,0:T(8,128)S(1)} %collective-permute-done.3.refs_1_) | copy-start | bytes 73732
  110.4 5.7 %collective-permute-start.8 = (f32[24,256]{1,0:T(8,128)}, f32[24,256]{1,0:T(8,128)S(1)}, u32[]{:S(2)}, u32[]{:S(2)}) collective-permute-start(f32[24,256]{1,0:T(8,128)} %get-tuple-element.35), channel_id=1, source_target_pairs={{0,6},{1,7},{2,0},{3,1},{4,2},{5,3},{6,4},{7,5},{8,14},{9,15},{10,... | collective-permute-start | bytes 73736 | tf_op jit(solution)/shard_map/ppermute | solution.py:306
  113.8 5.1 %copy-start.7 = (f32[24,256]{1,0:T(8,128)}, f32[24,256]{1,0:T(8,128)S(1)}, u32[]{:S(2)}) copy-start(f32[24,256]{1,0:T(8,128)S(1)} %collective-permute-done.4.refs_2_) | copy-start | bytes 73732
  113.8 5.0 %collective-permute-start.9 = (f32[24,256]{1,0:T(8,128)}, f32[24,256]{1,0:T(8,128)S(1)}, u32[]{:S(2)}, u32[]{:S(2)}) collective-permute-start(f32[24,256]{1,0:T(8,128)} %get-tuple-element.36), channel_id=1, source_target_pairs={{0,7},{1,0},{2,1},{3,2},{4,3},{5,4},{6,5},{7,6},{8,15},{9,8},{10,9... | collective-permute-start | bytes 73736 | tf_op jit(solution)/shard_map/ppermute | solution.py:306
  116.0 2.9 %copy-start.8 = (f32[24,256]{1,0:T(8,128)}, f32[24,256]{1,0:T(8,128)S(1)}, u32[]{:S(2)}) copy-start(f32[24,256]{1,0:T(8,128)S(1)} %collective-permute-done.5.refs_3_) | copy-start | bytes 73732
  116.0 2.8 %copy-start.9 = (f32[24,256]{1,0:T(8,128)}, f32[24,256]{1,0:T(8,128)S(1)}, u32[]{:S(2)}) copy-start(f32[24,256]{1,0:T(8,128)S(1)} %collective-permute-done.6.refs_4_) | copy-start | bytes 73732
  116.1 2.8 %copy-start.10 = (f32[24,256]{1,0:T(8,128)}, f32[24,256]{1,0:T(8,128)S(1)}, u32[]{:S(2)}) copy-start(f32[24,256]{1,0:T(8,128)S(1)} %collective-permute-done.7.refs_5_) | copy-start | bytes 73732
  116.1 2.8 %copy-start.11 = (f32[24,256]{1,0:T(8,128)}, f32[24,256]{1,0:T(8,128)S(1)}, u32[]{:S(2)}) copy-start(f32[24,256]{1,0:T(8,128)S(1)} %collective-permute-done.8.refs_6_) | copy-start | bytes 73732
  (2 other events, 1.2 us)

commit v4 on v2

--- a/solution.py
+++ b/solution.py
@@ -9,12 +9,14 @@
 
 HEADS = 8
 BLK = 128
+SMALL = 8 << 20
 MEAN_SCALE = 0.08838834764831845
 
 f32 = jnp.float32
 bf16 = jnp.bfloat16
 VMEM_SPEC = pl.BlockSpec(memory_space=pltpu.VMEM)
 SMEM_SPEC = pl.BlockSpec(memory_space=pltpu.SMEM)
+ANY_SPEC = pl.BlockSpec(memory_space=pl.ANY)
 
 
 def dot(a, b):
@@ -23,6 +25,10 @@
 
 def dot_nt(a, b):
     return lax.dot_general(a, b, (((1,), (1,)), ((), ())), preferred_element_type=f32)
+
+
+def dot_tt(a, b):
+    return lax.dot_general(a, b, (((0,), (1,)), ((), ())), preferred_element_type=f32)
 
 
 def dot_tn(a, b):
@@ -37,7 +43,6 @@
     wq_ref,
     wk_ref,
     wv_ref,
-    wkt_ref,
     back_ref,
     opg_ref,
     wgrad_ref,
@@ -45,17 +50,20 @@
     cm_ref,
     gq_ref,
     wkv_ref,
+    ct_ref,
 ):
     slots, blk, width = rows_ref.shape
     ops_count = op_ref.shape[0]
     head_size = width // HEADS
     inv_root = head_size ** (-0.5)
     d_scale = 0.25 * MEAN_SCALE * inv_root
-    pair = 2
+    pair = 8
     machines = pair * blk
+    steps = slots // pair
 
     queries = dot(op_ref[...], wq_ref[...]).astype(bf16)
     cot = cot_ref[...]
+    ct_ref[...] = cot.T
     lane_head = lax.broadcasted_iota(jnp.int32, (ops_count, width), 1) // head_size
     zero = jnp.zeros((), bf16)
     for h in range(HEADS):
@@ -70,13 +78,13 @@
         embed = rows_ref[pl.ds(first, pair)].reshape(machines, width)
         keys = dot(embed, wk_ref[...]).astype(bf16)
         values = dot(embed, wv_ref[...]).astype(bf16)
-        keys_t = dot_nt(wkt_ref[...], embed).astype(bf16)
+        keys_t = keys.T
         place = lax.broadcasted_iota(jnp.int32, (blk, ops_count), 0)
         eligible = jnp.concatenate(
             [place < counts_ref[first + s] for s in range(pair)], axis=0
         )
         key_grad = jnp.zeros((machines, width), f32)
-        value_grad = jnp.zeros((machines, width), f32)
+        value_grad = []
         for h in range(HEADS):
             q_h = qm_ref[pl.ds(h * ops_count, ops_count), :]
             c_h = cm_ref[pl.ds(h * ops_count, ops_count), :]
@@ -86,25 +94,26 @@
             gate2 = jnp.where(eligible, 1.0 + half, 0.0).astype(bf16)
             slope = jnp.where(eligible, value_dot * (1.0 - half * half), 0.0).astype(bf16)
             key_grad += dot(slope, q_h)
-            value_grad += dot(gate2, c_h)
+            value_grad.append(dot_nt(ct_ref[h * head_size : (h + 1) * head_size, :], gate2))
             gq_ref[pl.ds(h * head_size, head_size), :] += dot(
                 keys_t[h * head_size : (h + 1) * head_size, :], slope
             )
         key_grad = (key_grad * d_scale).astype(bf16)
-        value_grad = (value_grad * (0.5 * MEAN_SCALE)).astype(bf16)
-        back = dot_nt(key_grad, wk_ref[...]) + dot_nt(value_grad, wv_ref[...])
+        value_grad = (jnp.concatenate(value_grad, axis=0) * (0.5 * MEAN_SCALE)).astype(bf16)
+        back = dot_nt(key_grad, wk_ref[...]) + dot_tt(value_grad, wv_ref[...])
         back = back.astype(bf16)
         for s in range(pair):
             back_ref[first + s, 0:blk, :] = back[s * blk : (s + 1) * blk]
         wkv_ref[0:width, :] += dot_tn(embed, key_grad)
-        wkv_ref[width : 2 * width, :] += dot_tn(embed, value_grad)
+        wkv_ref[width : 2 * width, :] += dot(value_grad, embed)
         return carry
 
-    lax.fori_loop(0, slots // pair, one_pair, 0)
+    lax.fori_loop(0, steps, one_pair, 0)
     grad_query = (gq_ref[...] * d_scale).T.astype(bf16)
     opg_ref[...] = (cot.astype(f32) + dot_nt(grad_query, wq_ref[...])).astype(bf16)
     wgrad_ref[0:width, :] = dot_tn(op_ref[...], grad_query).astype(bf16)
-    wgrad_ref[width : 3 * width, :] = wkv_ref[...].astype(bf16)
+    wgrad_ref[width : 2 * width, :] = wkv_ref[0:width, :].astype(bf16)
+    wgrad_ref[2 * width : 3 * width, :] = wkv_ref[width : 2 * width, :].T.astype(bf16)
 
 
 def attend(rows, counts_t, op_embed, cotangent, w_query, w_key, w_value, extra=0):
@@ -112,7 +121,7 @@
     ops_count = op_embed.shape[0]
     return pl.pallas_call(
         attend_kernel,
-        in_specs=[VMEM_SPEC] * 8,
+        in_specs=[VMEM_SPEC] * 7,
         out_specs=[VMEM_SPEC] * 3,
         out_shape=[
             jax.ShapeDtypeStruct((slots, blk + extra, width), bf16),
@@ -124,7 +133,9 @@
             pltpu.VMEM((HEADS * ops_count, width), bf16),
             pltpu.VMEM((width, ops_count), f32),
             pltpu.VMEM((2 * width, width), f32),
+            pltpu.VMEM((width, ops_count), bf16),
         ],
+        compiler_params=pltpu.CompilerParams(vmem_limit_bytes=48 << 20),
         name="attend",
     )(
         rows,
@@ -134,21 +145,36 @@
         w_query,
         w_key,
         w_value,
-        w_key.T,
     )
 
 
-def pick_kernel(ids_ref, blocks_ref, out_ref):
-    for g in range(out_ref.shape[0]):
-        out_ref[g] = blocks_ref[ids_ref[g]]
+def pick_kernel(ids_ref, blocks_ref, out_ref, held, in_sem, out_sems):
+    load = pltpu.make_async_copy(blocks_ref, held, in_sem)
+    load.start()
+    load.wait()
+    copies = [
+        pltpu.make_async_copy(held.at[ids_ref[g, 0, 0]], out_ref.at[g], out_sems.at[g])
+        for g in range(out_ref.shape[0])
+    ]
+    for copy in copies:
+        copy.start()
+    for copy in copies:
+        copy.wait()
 
 
 def pick_blocks(ids, blocks):
+    groups = ids.shape[0]
     return pl.pallas_call(
         pick_kernel,
-        in_specs=[SMEM_SPEC, VMEM_SPEC],
-        out_specs=VMEM_SPEC,
-        out_shape=jax.ShapeDtypeStruct((ids.shape[0],) + blocks.shape[1:], blocks.dtype),
+        in_specs=[SMEM_SPEC, ANY_SPEC],
+        out_specs=ANY_SPEC,
+        out_shape=jax.ShapeDtypeStruct((groups,) + blocks.shape[1:], blocks.dtype),
+        scratch_shapes=[
+            pltpu.VMEM(blocks.shape, blocks.dtype),
+            pltpu.SemaphoreType.DMA,
+            pltpu.SemaphoreType.DMA((groups,)),
+        ],
+        compiler_params=pltpu.CompilerParams(vmem_limit_bytes=SMALL),
         name="pick_blocks",
     )(ids, blocks)
 
@@ -181,6 +207,7 @@
             pltpu.SemaphoreType.DMA((groups,)),
         ],
         input_output_aliases={1: 0},
+        compiler_params=pltpu.CompilerParams(vmem_limit_bytes=SMALL),
         name="fill_tail",
     )(parts, buffer)
 
@@ -194,7 +221,7 @@
     acc_ref[...] = jnp.zeros_like(acc_ref)
     total = jnp.zeros((lead, width), f32)
     for g in range(groups):
-        acc_ref[ids_ref[g]] += parts_ref[g, 0:blk, :].astype(f32)
+        acc_ref[ids_ref[g, 0, 0]] += parts_ref[g, 0:blk, :].astype(f32)
         total += parts_ref[g, blk : blk + lead, :].astype(f32)
     total = (total * (1.0 / (groups * shards))).astype(bf16)
     for s in range(shards):
@@ -214,6 +241,7 @@
         out_specs=VMEM_SPEC,
         out_shape=jax.ShapeDtypeStruct((shards, share + rows - BLK, width), bf16),
         scratch_shapes=[pltpu.VMEM((blocks, BLK, width), f32)],
+        compiler_params=pltpu.CompilerParams(vmem_limit_bytes=SMALL),
         name="collect_blocks",
     )(ids, parts)
 
@@ -245,6 +273,7 @@
         in_specs=[VMEM_SPEC],
         out_specs=[VMEM_SPEC] * 4,
         out_shape=[jax.ShapeDtypeStruct((share, width), f32), square, square, square],
+        compiler_params=pltpu.CompilerParams(vmem_limit_bytes=SMALL),
         name="finish",
     )(parts)
 
@@ -259,7 +288,7 @@
     width = op_embed.shape[1]
     machine_rows = machine_embed.shape[0]
     blocks_here = machine_rows // BLK
-    ids = swap(slot_local.reshape(groups, 1), "grp")[:, 0]
+    ids = swap(jnp.broadcast_to(slot_local.reshape(groups, 1, 1), (groups, 1, 128)), "grp")
     outgoing = pick_blocks(ids, machine_embed.reshape(blocks_here, BLK, width))
     rows = swap(outgoing, "grp")
     lead = 3 * width // shards

time: 173 us -> 155 us (0.90)
  Pallas kernels: 32.7 us -> 17.4 us
  blocking collectives: 105 us -> 103 us
    pallas_call x2, Pallas kernels: 26.4 us -> 15 us  [the longest x1 13.2 us: attend(): pl.pallas_call(attend_kernel, in_specs=[VMEM_SPEC] * 7, out_specs=[VMEM_S...]
  transfers between devices with their start and end apart: 1 -> 1, of which waited for: 1 -> 1; matrix products, arithmetic and copies ran while one was open for 1% -> 0% of each run, Pallas kernels for 0% -> 0%
where the time goes in v4:
time: 155 us
  blocking collectives  103 us (66%)
  waiting for transfers between devices  28 us (18%)
  Pallas kernels  17.4 us (11%)
  starting transfers between devices  4.25 us (3%)
  local copies, waits for them, and re-layouts  1.73 us (1%)
    all_to_all x4, blocking collectives, swap(): return lax.all_to_all(x, axis, split_axis=0, concat_axis=0, tiled=True)  103 us
    all_to_all x1, waiting for transfers between devices, swap(): return lax.all_to_all(x, axis, split_axis=0, concat_axis=0, tiled=True)  28 us
    pallas_call x1, Pallas kernels, attend(): pl.pallas_call(attend_kernel, in_specs=[VMEM_SPEC] * 7, out_specs=[VMEM_S...  13.2 us
    all_to_all x1, starting transfers between devices, swap(): return lax.all_to_all(x, axis, split_axis=0, concat_axis=0, tiled=True)  4.25 us
  transfers between devices with their start and end apart: 1, of which 1 were waited for; matrix products, arithmetic and copies ran while one was open for 0% of the time, Pallas kernels for 0%

profile of v4, /device:TPU:1, one launch (start us, length us, event | category | flops | bytes accessed | tf_op | source)
XLA Modules:
  0.0 155.0 jit_solution(17253814238606161527)
XLA Ops:
  0.6 0.7 broadcast_in_dim.8
  1.4 16.3 %all_to_all.25.ids_ref = s32[16,1,128]{2,1,0:T(1,128)S(1)} all-to-all(s32[16,1,128]{2,1,0:T(1,128)S(1)} %broadcast_in_dim.8), channel_id=1, replica_groups=mesh['grp'=16,'ops'=32] {'grp'}, dimensions={0} | all-to-all | bytes 16384 | tf_op jit(solution)/shard_map/all_to_all | solution.py:282
  17.7 0.9 copy-done
  18.6 1.8 %pick_blocks.1 = bf16[16,128,256]{2,1,0:T(8,128)(2,1)} custom-call(s32[16,1,128]{2,1,0:T(1,128)S(1)} %all_to_all.25.ids_ref, bf16[4,128,256]{2,1,0:T(8,128)(2,1)S(1)} %bitcast.5), custom_call_target="tpu_custom_call" | custom-call | tf_op jit(solution)/shard_map/pick_blocks/pallas_call | solution.py:167
  20.4 0.0 copy-start.6
  20.5 0.0 copy-start.1
  20.5 0.0 copy-start.2
  20.5 0.0 copy-start.3
  20.5 0.0 copy-start.4
  20.5 0.0 copy-start.5
  20.5 4.3 %all-to-all-start.1 = ((bf16[16,128,256]{2,1,0:T(8,128)(2,1)}), bf16[16,128,256]{2,1,0:T(8,128)(2,1)S(1)}, u32[]{:S(2)}, u32[]{:S(2)}) async-start(bf16[16,128,256]{2,1,0:T(8,128)(2,1)} %pick_blocks.1), calls=%async_computation.1 | async-start | bytes 2097152 | tf_op jit(solution)/shard_map/all_to_all | solution.py:282
  24.8 0.0 copy-done.6
  24.8 28.0 %all-to-all-done.1.rows_ref = bf16[16,128,256]{2,1,0:T(8,128)(2,1)S(1)} async-done(((bf16[16,128,256]{2,1,0:T(8,128)(2,1)}), bf16[16,128,256]{2,1,0:T(8,128)(2,1)S(1)}, u32[]{:S(2)}, u32[]{:S(2)}) %all-to-all-start.1) | async-done | bytes 1048608 | tf_op jit(solution)/shard_map/all_to_all | solution.py:282
  52.8 0.0 copy-done.1
  52.8 0.0 copy-done.2
  52.8 0.0 copy-done.3
  52.8 0.0 copy-done.4
  52.8 13.2 %attend.1 = (bf16[16,152,256]{2,1,0:T(8,128)(2,1)S(1)}, bf16[256,256]{1,0:T(8,128)(2,1)}, bf16[768,256]{1,0:T(8,128)(2,1)S(1)}) custom-call(bf16[16,128,256]{2,1,0:T(8,128)(2,1)S(1)} %all-to-all-done.1.rows_ref, s32[16,1,256]{2,1,0:T(1,128)S(1)} %reshape.24.counts_ref, bf16[256,256]{1,0:T(8,128)(2,1)S(1)} %copy-done.1, bf16[256,256]{1,0:T(8,128)(2,1)S(1)} %copy-done.2, ...), custom_call_target="tpu_custom_call" | custom-call | tf_op jit(solution)/shard_map/attend/pallas_call | solution.py:122
  66.0 25.7 %all_to_all.26.parts_ref = bf16[32,24,256]{2,1,0:T(8,128)(2,1)S(1)} all-to-all(bf16[32,24,256]{2,1,0:T(8,128)(2,1)S(1)} %bitcast.4), channel_id=1, replica_groups=mesh['grp'=16,'ops'=32] {'ops'}, dimensions={0} | all-to-all | bytes 786432 | tf_op jit(solution)/shard_map/all_to_all | solution.py:282
  91.7 0.5 fill_tail.1
  92.2 36.7 %all_to_all.27.parts_ref = bf16[16,152,256]{2,1,0:T(8,128)(2,1)S(1)} all-to-all(bf16[16,152,256]{2,1,0:T(8,128)(2,1)S(1)} %fill_tail.1), channel_id=1, replica_groups=mesh['grp'=16,'ops'=32] {'grp'}, dimensions={0} | all-to-all | bytes 2490368 | tf_op jit(solution)/shard_map/all_to_all | solution.py:282
  128.9 1.0 collect_blocks.1
  129.9 24.2 %all_to_all.28.parts_ref = bf16[32,40,256]{2,1,0:T(8,128)(2,1)S(1)} all-to-all(bf16[32,40,256]{2,1,0:T(8,128)(2,1)S(1)} %collect_blocks.1), channel_id=1, replica_groups=mesh['grp'=16,'ops'=32] {'ops'}, dimensions={0} | all-to-all | bytes 1310720 | tf_op jit(solution)/shard_map/all_to_all | solution.py:282
  154.1 0.9 finish.1
  (3 shorter events, 0.0 us)
Async XLA Ops:
  17.7 1.0 copy-start
  20.4 4.3 %copy-start.6 = (s32[256,16]{0,1:T(8,128)S(1)}, s32[256,16]{0,1:T(8,128)}, u32[]{:S(2)}) copy-start(s32[256,16]{0,1:T(8,128)} %param.15) | copy-start | bytes 49156
  20.5 32.4 %copy-start.1 = (bf16[256,256]{1,0:T(8,128)(2,1)S(1)}, bf16[256,256]{1,0:T(8,128)(2,1)}, u32[]{:S(2)}) copy-start(bf16[256,256]{1,0:T(8,128)(2,1)} %op_ref.1) | copy-start | bytes 393220
  20.5 32.4 %copy-start.2 = (bf16[256,256]{1,0:T(8,128)(2,1)S(1)}, bf16[256,256]{1,0:T(8,128)(2,1)}, u32[]{:S(2)}) copy-start(bf16[256,256]{1,0:T(8,128)(2,1)} %cot_ref.1) | copy-start | bytes 393220
  20.5 32.3 %copy-start.3 = (bf16[256,256]{1,0:T(8,128)(2,1)S(1)}, bf16[256,256]{1,0:T(8,128)(2,1)}, u32[]{:S(2)}) copy-start(bf16[256,256]{1,0:T(8,128)(2,1)} %wq_ref.1) | copy-start | bytes 393220
  20.5 32.3 %copy-start.4 = (bf16[256,256]{1,0:T(8,128)(2,1)S(1)}, bf16[256,256]{1,0:T(8,128)(2,1)}, u32[]{:S(2)}) copy-start(bf16[256,256]{1,0:T(8,128)(2,1)} %wk_ref.1) | copy-start | bytes 393220
  20.5 32.3 %copy-start.5 = (bf16[256,256]{1,0:T(8,128)(2,1)S(1)}, bf16[256,256]{1,0:T(8,128)(2,1)}, u32[]{:S(2)}) copy-start(bf16[256,256]{1,0:T(8,128)(2,1)} %wv_ref.1) | copy-start | bytes 393220
  20.5 32.3 %all-to-all-start.1 = ((bf16[16,128,256]{2,1,0:T(8,128)(2,1)}), bf16[16,128,256]{2,1,0:T(8,128)(2,1)S(1)}, u32[]{:S(2)}, u32[]{:S(2)}) async-start(bf16[16,128,256]{2,1,0:T(8,128)(2,1)} %pick_blocks.1), calls=%async_computation.1 | async-start | bytes 2097152 | tf_op jit(solution)/shard_map/all_to_all | solution.py:282

commit v5 on v4

--- a/solution.py
+++ b/solution.py
@@ -57,7 +57,7 @@
     head_size = width // HEADS
     inv_root = head_size ** (-0.5)
     d_scale = 0.25 * MEAN_SCALE * inv_root
-    pair = 8
+    pair = 16
     machines = pair * blk
     steps = slots // pair
 
@@ -174,7 +174,7 @@
             pltpu.SemaphoreType.DMA,
             pltpu.SemaphoreType.DMA((groups,)),
         ],
-        compiler_params=pltpu.CompilerParams(vmem_limit_bytes=SMALL),
+        compiler_params=pltpu.CompilerParams(vmem_limit_bytes=60 << 20),
         name="pick_blocks",
     )(ids, blocks)
 

time: 155 us -> 155 us (level)
  no operation moved by 1% of the time
where the time goes in v5:
time: 155 us
  blocking collectives  103 us (66%)
  waiting for transfers between devices  28 us (18%)
  Pallas kernels  17.9 us (12%)
  starting transfers between devices  4.1 us (3%)
    all_to_all x4, blocking collectives, swap(): return lax.all_to_all(x, axis, split_axis=0, concat_axis=0, tiled=True)  103 us
    all_to_all x1, waiting for transfers between devices, swap(): return lax.all_to_all(x, axis, split_axis=0, concat_axis=0, tiled=True)  28 us
    pallas_call x1, Pallas kernels, attend(): pl.pallas_call(attend_kernel, in_specs=[VMEM_SPEC] * 7, out_specs=[VMEM_S...  12.7 us
    all_to_all x1, starting transfers between devices, swap(): return lax.all_to_all(x, axis, split_axis=0, concat_axis=0, tiled=True)  4.1 us
  transfers between devices with their start and end apart: 1, of which 1 were waited for; matrix products, arithmetic and copies ran while one was open for 0% of the time, Pallas kernels for 0%

profile of v5, /device:TPU:1, one launch (start us, length us, event | category | flops | bytes accessed | tf_op | source)
XLA Modules:
  0.0 154.6 jit_solution(9373682296911717936)
XLA Ops:
  0.6 0.7 broadcast_in_dim.8
  1.4 16.9 %all_to_all.25.ids_ref = s32[16,1,128]{2,1,0:T(1,128)} all-to-all(s32[16,1,128]{2,1,0:T(1,128)S(1)} %broadcast_in_dim.8), channel_id=1, replica_groups=mesh['grp'=16,'ops'=32] {'grp'}, dimensions={0} | all-to-all | bytes 16384 | tf_op jit(solution)/shard_map/all_to_all | solution.py:282
  18.3 2.9 %pick_blocks.1 = bf16[16,128,256]{2,1,0:T(8,128)(2,1)} custom-call(s32[16,1,128]{2,1,0:T(1,128)} %all_to_all.25.ids_ref, bf16[4,128,256]{2,1,0:T(8,128)(2,1)} %bitcast.5), custom_call_target="tpu_custom_call" | custom-call | tf_op jit(solution)/shard_map/pick_blocks/pallas_call | solution.py:167
  21.2 0.0 copy-start.6
  21.2 0.0 copy-start
  21.2 0.0 copy-start.1
  21.2 0.0 copy-start.2
  21.2 0.0 copy-start.3
  21.2 0.0 copy-start.4
  21.3 4.1 %all-to-all-start.1 = ((bf16[16,128,256]{2,1,0:T(8,128)(2,1)}), bf16[16,128,256]{2,1,0:T(8,128)(2,1)S(1)}, u32[]{:S(2)}, u32[]{:S(2)}) async-start(bf16[16,128,256]{2,1,0:T(8,128)(2,1)} %pick_blocks.1), calls=%async_computation.1 | async-start | bytes 2097152 | tf_op jit(solution)/shard_map/all_to_all | solution.py:282
  25.4 0.0 copy-done.6
  25.4 28.0 %all-to-all-done.1.rows_ref = bf16[16,128,256]{2,1,0:T(8,128)(2,1)S(1)} async-done(((bf16[16,128,256]{2,1,0:T(8,128)(2,1)}), bf16[16,128,256]{2,1,0:T(8,128)(2,1)S(1)}, u32[]{:S(2)}, u32[]{:S(2)}) %all-to-all-start.1) | async-done | bytes 1048608 | tf_op jit(solution)/shard_map/all_to_all | solution.py:282
  53.4 0.0 copy-done
  53.4 0.0 copy-done.1
  53.4 0.0 copy-done.2
  53.4 0.0 copy-done.3
  53.4 12.7 %attend.1 = (bf16[16,152,256]{2,1,0:T(8,128)(2,1)S(1)}, bf16[256,256]{1,0:T(8,128)(2,1)}, bf16[768,256]{1,0:T(8,128)(2,1)S(1)}) custom-call(bf16[16,128,256]{2,1,0:T(8,128)(2,1)S(1)} %all-to-all-done.1.rows_ref, s32[16,1,256]{2,1,0:T(1,128)S(1)} %reshape.24.counts_ref, bf16[256,256]{1,0:T(8,128)(2,1)S(1)} %copy-done, bf16[256,256]{1,0:T(8,128)(2,1)S(1)} %copy-done.1, ...), custom_call_target="tpu_custom_call" | custom-call | tf_op jit(solution)/shard_map/attend/pallas_call | solution.py:122
  66.1 25.1 %all_to_all.26.parts_ref = bf16[32,24,256]{2,1,0:T(8,128)(2,1)S(1)} all-to-all(bf16[32,24,256]{2,1,0:T(8,128)(2,1)S(1)} %bitcast.4), channel_id=1, replica_groups=mesh['grp'=16,'ops'=32] {'ops'}, dimensions={0} | all-to-all | bytes 786432 | tf_op jit(solution)/shard_map/all_to_all | solution.py:282
  91.3 0.5 fill_tail.1
  91.8 36.7 %all_to_all.27.parts_ref = bf16[16,152,256]{2,1,0:T(8,128)(2,1)S(1)} all-to-all(bf16[16,152,256]{2,1,0:T(8,128)(2,1)S(1)} %fill_tail.1), channel_id=1, replica_groups=mesh['grp'=16,'ops'=32] {'grp'}, dimensions={0} | all-to-all | bytes 2490368 | tf_op jit(solution)/shard_map/all_to_all | solution.py:282
  128.5 0.0 copy-done.5
  128.5 0.9 collect_blocks.1
  129.5 24.2 %all_to_all.28.parts_ref = bf16[32,40,256]{2,1,0:T(8,128)(2,1)S(1)} all-to-all(bf16[32,40,256]{2,1,0:T(8,128)(2,1)S(1)} %collect_blocks.1), channel_id=1, replica_groups=mesh['grp'=16,'ops'=32] {'ops'}, dimensions={0} | all-to-all | bytes 1310720 | tf_op jit(solution)/shard_map/all_to_all | solution.py:282
  153.7 0.9 finish.1
  (3 shorter events, 0.0 us)
Async XLA Ops:
  21.2 4.2 %copy-start.6 = (s32[256,16]{0,1:T(8,128)S(1)}, s32[256,16]{0,1:T(8,128)}, u32[]{:S(2)}) copy-start(s32[256,16]{0,1:T(8,128)} %param.15) | copy-start | bytes 49156
  21.2 32.2 %copy-start = (bf16[256,256]{1,0:T(8,128)(2,1)S(1)}, bf16[256,256]{1,0:T(8,128)(2,1)}, u32[]{:S(2)}) copy-start(bf16[256,256]{1,0:T(8,128)(2,1)} %op_ref.1) | copy-start | bytes 393220
  21.2 32.2 %copy-start.1 = (bf16[256,256]{1,0:T(8,128)(2,1)S(1)}, bf16[256,256]{1,0:T(8,128)(2,1)}, u32[]{:S(2)}) copy-start(bf16[256,256]{1,0:T(8,128)(2,1)} %cot_ref.1) | copy-start | bytes 393220
  21.2 32.2 %copy-start.2 = (bf16[256,256]{1,0:T(8,128)(2,1)S(1)}, bf16[256,256]{1,0:T(8,128)(2,1)}, u32[]{:S(2)}) copy-start(bf16[256,256]{1,0:T(8,128)(2,1)} %wq_ref.1) | copy-start | bytes 393220
  21.2 32.2 %copy-start.3 = (bf16[256,256]{1,0:T(8,128)(2,1)S(1)}, bf16[256,256]{1,0:T(8,128)(2,1)}, u32[]{:S(2)}) copy-start(bf16[256,256]{1,0:T(8,128)(2,1)} %wk_ref.1) | copy-start | bytes 393220
  21.2 32.2 %copy-start.4 = (bf16[256,256]{1,0:T(8,128)(2,1)S(1)}, bf16[256,256]{1,0:T(8,128)(2,1)}, u32[]{:S(2)}) copy-start(bf16[256,256]{1,0:T(8,128)(2,1)} %wv_ref.1) | copy-start | bytes 393220
  21.3 32.1 %all-to-all-start.1 = ((bf16[16,128,256]{2,1,0:T(8,128)(2,1)}), bf16[16,128,256]{2,1,0:T(8,128)(2,1)S(1)}, u32[]{:S(2)}, u32[]{:S(2)}) async-start(bf16[16,128,256]{2,1,0:T(8,128)(2,1)} %pick_blocks.1), calls=%async_computation.1 | async-start | bytes 2097152 | tf_op jit(solution)/shard_map/all_to_all | solution.py:282
  91.8 36.7 %copy-start.5 = (s32[16,1,128]{2,1,0:T(1,128)S(1)}, s32[16,1,128]{2,1,0:T(1,128)}, u32[]{:S(2)}) copy-start(s32[16,1,128]{2,1,0:T(1,128)} %all_to_all.25.ids_ref) | copy-start | bytes 24580

commit v6 on v5

--- a/solution.py
+++ b/solution.py
@@ -81,7 +81,7 @@
         keys_t = keys.T
         place = lax.broadcasted_iota(jnp.int32, (blk, ops_count), 0)
         eligible = jnp.concatenate(
-            [place < counts_ref[first + s] for s in range(pair)], axis=0
+            [place < counts_ref[first + s : first + s + 1, :] for s in range(pair)], axis=0
         )
         key_grad = jnp.zeros((machines, width), f32)
         value_grad = []
@@ -108,7 +108,8 @@
         wkv_ref[width : 2 * width, :] += dot(value_grad, embed)
         return carry
 
-    lax.fori_loop(0, steps, one_pair, 0)
+    for step in range(steps):
+        one_pair(step, 0)
     grad_query = (gq_ref[...] * d_scale).T.astype(bf16)
     opg_ref[...] = (cot.astype(f32) + dot_nt(grad_query, wq_ref[...])).astype(bf16)
     wgrad_ref[0:width, :] = dot_tn(op_ref[...], grad_query).astype(bf16)
@@ -139,7 +140,7 @@
         name="attend",
     )(
         rows,
-        counts_t.reshape(slots, 1, ops_count),
+        counts_t,
         op_embed,
         cotangent,
         w_query,
@@ -148,33 +149,19 @@
     )
 
 
-def pick_kernel(ids_ref, blocks_ref, out_ref, held, in_sem, out_sems):
-    load = pltpu.make_async_copy(blocks_ref, held, in_sem)
-    load.start()
-    load.wait()
-    copies = [
-        pltpu.make_async_copy(held.at[ids_ref[g, 0, 0]], out_ref.at[g], out_sems.at[g])
-        for g in range(out_ref.shape[0])
-    ]
-    for copy in copies:
-        copy.start()
-    for copy in copies:
-        copy.wait()
+def pick_kernel(ids_ref, blocks_ref, out_ref):
+    for g in range(out_ref.shape[0]):
+        out_ref[g] = blocks_ref[ids_ref[g, 0, 0]]
 
 
 def pick_blocks(ids, blocks):
     groups = ids.shape[0]
     return pl.pallas_call(
         pick_kernel,
-        in_specs=[SMEM_SPEC, ANY_SPEC],
-        out_specs=ANY_SPEC,
+        in_specs=[SMEM_SPEC, VMEM_SPEC],
+        out_specs=VMEM_SPEC,
         out_shape=jax.ShapeDtypeStruct((groups,) + blocks.shape[1:], blocks.dtype),
-        scratch_shapes=[
-            pltpu.VMEM(blocks.shape, blocks.dtype),
-            pltpu.SemaphoreType.DMA,
-            pltpu.SemaphoreType.DMA((groups,)),
-        ],
-        compiler_params=pltpu.CompilerParams(vmem_limit_bytes=60 << 20),
+        compiler_params=pltpu.CompilerParams(vmem_limit_bytes=SMALL),
         name="pick_blocks",
     )(ids, blocks)
 

time: 155 us -> 153 us (0.987)
  blocking collectives: 103 us -> 134 us
  waiting for transfers between devices: 28 us -> 0 us
  starting transfers between devices: 4.1 us -> 0 us
  Pallas kernels: 17.9 us -> 15.8 us
    all_to_all x4 -> x5, blocking collectives: 103 us -> 134 us  [swap(): return lax.all_to_all(x, axis, split_axis=0, concat_axis=0, tiled=True)]
    all_to_all x1 -> x0, waiting for transfers between devices: 28 us -> none  [swap(): return lax.all_to_all(x, axis, split_axis=0, concat_axis=0, tiled=True)]
    all_to_all x1 -> x0, starting transfers between devices: 4.1 us -> none  [swap(): return lax.all_to_all(x, axis, split_axis=0, concat_axis=0, tiled=True)]
    pallas_call x1, Pallas kernels: 2.86 us -> 0.74 us  [pick_blocks(): pl.pallas_call(pick_kernel, in_specs=[SMEM_SPEC, VMEM_SPEC], out_specs=VM...]
  transfers between devices with their start and end apart: 1 -> 0, of which waited for: 1 -> 0; matrix products, arithmetic and copies ran while one was open for 0% -> 0% of each run, Pallas kernels for 0% -> 0%
where the time goes in v6:
time: 153 us; the launch traced here: 152 us
  blocking collectives  134 us (88%)
  Pallas kernels  15.8 us (10%)
  local copies, waits for them, and re-layouts  1.72 us (1%)
    all_to_all x5, blocking collectives, swap(): return lax.all_to_all(x, axis, split_axis=0, concat_axis=0, tiled=True)  134 us
    pallas_call x1, Pallas kernels, attend(): pl.pallas_call(attend_kernel, in_specs=[VMEM_SPEC] * 7, out_specs=[VMEM_S...  12.7 us

profile of v6, /device:TPU:1, one launch (start us, length us, event | category | flops | bytes accessed | tf_op | source)
XLA Modules:
  0.0 152.5 jit_solution(12676006640976920018)
XLA Ops:
  0.6 0.7 broadcast_in_dim.8
  1.4 16.3 %all_to_all.25.ids_ref = s32[16,1,128]{2,1,0:T(1,128)S(1)} all-to-all(s32[16,1,128]{2,1,0:T(1,128)S(1)} %broadcast_in_dim.8), channel_id=1, replica_groups=mesh['grp'=16,'ops'=32] {'grp'}, dimensions={0} | all-to-all | bytes 16384 | tf_op jit(solution)/shard_map/all_to_all | solution.py:269
  17.7 0.9 copy-done
  18.6 0.7 pick_blocks.1
  19.4 0.0 copy-start.1
  19.4 0.0 copy-start.2
  19.4 0.0 copy-start.3
  19.4 0.0 copy-start.4
  19.4 0.0 copy-start.5
  19.4 0.0 copy-start.6
  19.4 31.8 %all_to_all.26.rows_ref = bf16[16,128,256]{2,1,0:T(8,128)(2,1)S(1)} all-to-all(bf16[16,128,256]{2,1,0:T(8,128)(2,1)S(1)} %pick_blocks.1), channel_id=1, replica_groups=mesh['grp'=16,'ops'=32] {'grp'}, dimensions={0} | all-to-all | bytes 2097152 | tf_op jit(solution)/shard_map/all_to_all | solution.py:269
  51.2 0.0 copy-done.1
  51.2 0.0 copy-done.2
  51.2 0.0 copy-done.3
  51.2 0.0 copy-done.4
  51.2 0.0 copy-done.5
  51.3 0.0 copy-done.6
  51.3 12.7 %attend.1 = (bf16[16,152,256]{2,1,0:T(8,128)(2,1)S(1)}, bf16[256,256]{1,0:T(8,128)(2,1)}, bf16[768,256]{1,0:T(8,128)(2,1)S(1)}) custom-call(bf16[16,128,256]{2,1,0:T(8,128)(2,1)S(1)} %all_to_all.26.rows_ref, s32[16,256]{1,0:T(8,128)S(1)} %bitcast.6, bf16[256,256]{1,0:T(8,128)(2,1)S(1)} %copy-done.1, bf16[256,256]{1,0:T(8,128)(2,1)S(1)} %copy-done.2, ...), custom_call_target="tpu_custom_call" | custom-call | tf_op jit(solution)/shard_map/attend/pallas_call | solution.py:123
  64.0 25.7 %all_to_all.27.parts_ref = bf16[32,24,256]{2,1,0:T(8,128)(2,1)S(1)} all-to-all(bf16[32,24,256]{2,1,0:T(8,128)(2,1)S(1)} %bitcast.4), channel_id=1, replica_groups=mesh['grp'=16,'ops'=32] {'ops'}, dimensions={0} | all-to-all | bytes 786432 | tf_op jit(solution)/shard_map/all_to_all | solution.py:269
  89.7 0.5 fill_tail.1
  90.2 36.2 %all_to_all.28.parts_ref = bf16[16,152,256]{2,1,0:T(8,128)(2,1)S(1)} all-to-all(bf16[16,152,256]{2,1,0:T(8,128)(2,1)S(1)} %fill_tail.1), channel_id=1, replica_groups=mesh['grp'=16,'ops'=32] {'grp'}, dimensions={0} | all-to-all | bytes 2490368 | tf_op jit(solution)/shard_map/all_to_all | solution.py:269
  126.4 1.0 collect_blocks.1
  127.4 24.2 %all_to_all.29.parts_ref = bf16[32,40,256]{2,1,0:T(8,128)(2,1)S(1)} all-to-all(bf16[32,40,256]{2,1,0:T(8,128)(2,1)S(1)} %collect_blocks.1), channel_id=1, replica_groups=mesh['grp'=16,'ops'=32] {'ops'}, dimensions={0} | all-to-all | bytes 1310720 | tf_op jit(solution)/shard_map/all_to_all | solution.py:269
  151.5 0.9 finish.1
  (1 shorter events, 0.0 us)
Async XLA Ops:
  17.7 1.0 copy-start
  19.4 31.9 %copy-start.1 = (bf16[256,256]{1,0:T(8,128)(2,1)S(1)}, bf16[256,256]{1,0:T(8,128)(2,1)}, u32[]{:S(2)}) copy-start(bf16[256,256]{1,0:T(8,128)(2,1)} %op_ref.1) | copy-start | bytes 393220
  19.4 31.9 %copy-start.2 = (bf16[256,256]{1,0:T(8,128)(2,1)S(1)}, bf16[256,256]{1,0:T(8,128)(2,1)}, u32[]{:S(2)}) copy-start(bf16[256,256]{1,0:T(8,128)(2,1)} %cot_ref.1) | copy-start | bytes 393220
  19.4 31.8 %copy-start.3 = (bf16[256,256]{1,0:T(8,128)(2,1)S(1)}, bf16[256,256]{1,0:T(8,128)(2,1)}, u32[]{:S(2)}) copy-start(bf16[256,256]{1,0:T(8,128)(2,1)} %wq_ref.1) | copy-start | bytes 393220
  19.4 31.8 %copy-start.4 = (bf16[256,256]{1,0:T(8,128)(2,1)S(1)}, bf16[256,256]{1,0:T(8,128)(2,1)}, u32[]{:S(2)}) copy-start(bf16[256,256]{1,0:T(8,128)(2,1)} %wk_ref.1) | copy-start | bytes 393220
  19.4 31.8 %copy-start.5 = (bf16[256,256]{1,0:T(8,128)(2,1)S(1)}, bf16[256,256]{1,0:T(8,128)(2,1)}, u32[]{:S(2)}) copy-start(bf16[256,256]{1,0:T(8,128)(2,1)} %wv_ref.1) | copy-start | bytes 393220
  19.4 31.8 %copy-start.6 = (s32[256,16]{0,1:T(8,128)S(1)}, s32[256,16]{0,1:T(8,128)}, u32[]{:S(2)}) copy-start(s32[256,16]{0,1:T(8,128)} %param.15) | copy-start | bytes 49156
